TPU v7x, 128 devices: a whole 4x4x4 slice. The times are simulated.
128 devices in a mesh: ta: 4 (over y), gx: 32 (over x, z, core).
Axes of the slice: x: 4, y: 4, z: 4, core: 2. Of those that a mesh axis runs over, the one named last changes fastest.
Arguments:
- eigvecs: bfloat16 [4, 16384, 3, 2, 384], P('ta', 'gx'), may hold values from -0.01953125 to 0.01953125
- perambulators: bfloat16 [4, 2, 384, 4, 4, 384], P('ta', None, 'gx'), may hold values from -0.59765625 to 0.59765625
- source_blocks: bfloat16 [9, 2, 384, 384], replicated, may hold values from -0.3125 to 0.3125
- momenta: int32 [9, 3], replicated, may hold values from -2 to 2
- op_momentum: int32 [64], replicated, may hold values from 0 to 8
- op_gamma: int32 [64], replicated, may hold values from 0 to 15
- ref_vectors: float32 [2, 64, 8], replicated, may hold values from -0.75 to 0.75
Outputs:
- correlator: float32 [4, 2, 64, 64], P('ta')
- projected: float32 [4, 2, 8, 8], P('ta')
All inputs are finite; a program needn't handle non-finite values.
Results may differ from a plain program's by a relative error of at most 0.0055.
Values may be sent and summed in bfloat16 or wider, within the bound.
No kernel may reach another device: no remote copies, remote signals or barrier semaphores. Data moves between devices by JAX's collectives and lax.ppermute only.
A program may use at most 128 MiB of HBM per device.

v0:
```python
import math

import jax
import jax.numpy as jnp
import numpy as np
from jax import lax
from jax.sharding import PartitionSpec as P

EXTENT = 96
NMOM = 9


full_precision = lax.Precision.HIGHEST


def cut_along(shard, dim, length):
    dims = shard.shape
    pieces = shard.reshape(*dims[:dim], length, dims[dim] // length, *dims[dim + 1 :])
    return jnp.moveaxis(pieces, dim, 0)


def sent_and_summed(shard, axis, dim):
    length = lax.axis_size(axis)
    pieces = lax.all_to_all(cut_along(shard, dim, length), axis, 0, 0, tiled=True)
    return jnp.sum(pieces, axis=0)


def from_everyone(shard, axis):
    length = lax.axis_size(axis)
    return lax.all_to_all(
        jnp.broadcast_to(shard[None], (length, *shard.shape)), axis, 0, 0, tiled=True
    )


def taken_together(shard, axis):
    everything = from_everyone(shard, axis)
    return jnp.sum(everything, axis=0)


def together(arrays, axis):
    flat, at, done = (jnp.concatenate([a.reshape(-1) for a in arrays]), 0, [])
    so_far = taken_together(flat, axis)
    for a in arrays:
        done.append(so_far[at : at + a.size].reshape(a.shape))
        at += a.size
    return tuple(done)


def picked(shard, axis, root):
    return lax.dynamic_index_in_dim(lax.all_gather(shard, axis), root, 0, keepdims=False)


def gamma_tables():
    zero_block = np.zeros((4, 4), np.float32)
    first_imag = np.array([[0, 0, 0, 1], [0, 0, 1, 0], [0, -1, 0, 0], [-1, 0, 0, 0]], np.float32)
    second_real = np.array([[0, 0, 0, -1], [0, 0, 1, 0], [0, 1, 0, 0], [-1, 0, 0, 0]], np.float32)
    third_imag = np.array([[0, 0, 1, 0], [0, 0, 0, -1], [-1, 0, 0, 0], [0, 1, 0, 0]], np.float32)
    fourth_real = np.array([[0, 0, 1, 0], [0, 0, 0, 1], [1, 0, 0, 0], [0, 1, 0, 0]], np.float32)
    gamma_list = [
        (zero_block, first_imag),
        (second_real, zero_block),
        (zero_block, third_imag),
        (fourth_real, zero_block),
    ]
    real_parts = []
    imag_parts = []
    for subset in range(16):
        prod_real = np.eye(4, dtype=np.float32)
        prod_imag = np.zeros((4, 4), np.float32)
        for position in range(4):
            if subset >> position & 1:
                factor_real, factor_imag = gamma_list[position]
                prod_real, prod_imag = (
                    prod_real @ factor_real - prod_imag @ factor_imag,
                    prod_real @ factor_imag + prod_imag @ factor_real,
                )
        real_parts.append(prod_real)
        imag_parts.append(prod_imag)
    return (np.stack(real_parts).astype(np.float32), np.stack(imag_parts).astype(np.float32))


def complex_einsum(form, left_real, left_imag, right_real, right_imag):

    def single(left_part, right_part):
        return jnp.einsum(
            form,
            left_part,
            right_part,
            precision=full_precision,
            preferred_element_type=jnp.float32,
        )

    return (
        single(left_real, right_real) - single(left_imag, right_imag),
        single(left_real, right_imag) + single(left_imag, right_real),
    )


def phase_factors(momenta, site_ids):
    xcoord = site_ids % EXTENT
    ycoord = site_ids // EXTENT % EXTENT
    zcoord = site_ids // (EXTENT * EXTENT)
    winding = (
        momenta[:, 0:1] * xcoord[None, :]
        + momenta[:, 1:2] * ycoord[None, :]
        + momenta[:, 2:3] * zcoord[None, :]
    ) % EXTENT
    phase_angle = winding.astype(jnp.float32) * (-2.0 * math.pi / EXTENT)
    return (jnp.cos(phase_angle), jnp.sin(phase_angle))


def right_block(vec_real, vec_imag, cosine, sine_row):
    cosine = cosine[:, None, None]
    sine_row = sine_row[:, None, None]
    eig_width = vec_real.shape[-1]
    twist_real = (
        (cosine * vec_real - sine_row * vec_imag).astype(jnp.bfloat16).reshape(-1, eig_width)
    )
    twist_imag = (
        (cosine * vec_imag + sine_row * vec_real).astype(jnp.bfloat16).reshape(-1, eig_width)
    )
    upper = jnp.concatenate([twist_real, twist_imag], 1)
    lower = jnp.concatenate([twist_imag, -twist_real], 1)
    return jnp.concatenate([upper, lower], 0)


def assemble(blocks_real, blocks_imag, op_momentum, op_gamma):
    table_real, table_imag = gamma_tables()
    chosen = (op_gamma[:, None] == jnp.arange(16, dtype=jnp.int32)[None, :]).astype(jnp.float32)
    gre = jnp.einsum("ig,gax->iax", chosen, jnp.asarray(table_real), precision=full_precision)
    gim = jnp.einsum("ig,gax->iax", chosen, jnp.asarray(table_imag), precision=full_precision)
    moment = (op_momentum[:, None] == jnp.arange(NMOM, dtype=jnp.int32)[None, :]).astype(
        jnp.float32
    )
    chiral = jnp.asarray(np.array([1.0, 1.0, -1.0, -1.0], np.float32))
    weight_left = moment[:, :, None, None] * chiral[None, None, None, :]
    left_real = weight_left * jnp.transpose(gre, (0, 2, 1))[:, None]
    left_imag = weight_left * jnp.transpose(gim, (0, 2, 1))[:, None]
    lifted_real, lifted_imag = complex_einsum(
        "imxa,mxynwa->iynw", left_real, left_imag, blocks_real, blocks_imag
    )
    weight_right = moment[:, :, None, None] * chiral[None, None, None, :]
    right_real = weight_right * jnp.transpose(gre, (0, 2, 1))[:, None]
    right_imag = -weight_right * jnp.transpose(gim, (0, 2, 1))[:, None]
    return complex_einsum("iynw,jnyw->ij", lifted_real, lifted_imag, right_real, right_imag)


def project(corr_real, corr_imag, ref_vectors):
    basis_real = ref_vectors[0]
    basis_imag = ref_vectors[1]
    half_real, half_imag = complex_einsum("ij,jv->iv", corr_real, corr_imag, basis_real, basis_imag)
    return complex_einsum("iu,iv->uv", basis_real, -basis_imag, half_real, half_imag)


def transpose_product(conj_left, twist_right):
    return lax.dot_general(
        conj_left, twist_right, (((0,), (0,)), ((), ())), preferred_element_type=jnp.float32
    )


def body(eigvecs, perambulators, source_blocks, momenta, op_momentum, op_gamma, ref_vectors):
    vectors = eigvecs[0]
    sites_here = vectors.shape[0]
    eig_width = vectors.shape[-1]
    vec_real = vectors[:, :, 0, :]
    vec_imag = vectors[:, :, 1, :]
    site_ids = lax.axis_index("gx") * sites_here + jnp.arange(sites_here, dtype=jnp.int32)
    cosine, sine_row = phase_factors(momenta, site_ids)
    conj_left = jnp.concatenate(
        [vec_real.reshape(-1, eig_width), vec_imag.reshape(-1, eig_width)], 0
    )
    row_count = eig_width // lax.axis_size("gx")
    pieces = []
    for moment_index in range(NMOM):
        twist_right = right_block(vec_real, vec_imag, cosine[moment_index], sine_row[moment_index])
        summed = sent_and_summed(transpose_product(conj_left, twist_right), "gx", 0)
        pieces.append(summed.reshape(row_count, 2, eig_width))
    phase_rows = jnp.stack(pieces, 1).astype(jnp.bfloat16)
    piece = lax.all_gather(perambulators, "gx", axis=2, tiled=True)
    new_real, new_imag = complex_einsum(
        "rml,labk->mrabk", phase_rows[:, :, 0], phase_rows[:, :, 1], piece[0, 0], piece[0, 1]
    )
    sink_real = new_real
    sink_imag = new_imag
    sink_real = sink_real.astype(jnp.bfloat16)
    sink_imag = sink_imag.astype(jnp.bfloat16)
    local_peram = perambulators[0]
    src_real, src_imag = complex_einsum(
        "rabl,nkl->rabnk", local_peram[0], -local_peram[1], source_blocks[:, 0], source_blocks[:, 1]
    )
    src_real = src_real.astype(jnp.bfloat16)
    src_imag = src_imag.astype(jnp.bfloat16)
    blocks_real, blocks_imag = complex_einsum(
        "mrxyk,rawnk->mxynwa", sink_real, sink_imag, src_real, src_imag
    )
    corr_real, corr_imag = assemble(blocks_real, blocks_imag, op_momentum, op_gamma)
    corr_real, corr_imag = together((corr_real, corr_imag), "gx")
    proj_real, proj_imag = project(corr_real, corr_imag, ref_vectors)
    raw_pair = jnp.stack([proj_real, proj_imag])
    local_square = jnp.mean(raw_pair * raw_pair)
    first_square = picked(local_square, "ta", 0)
    scale_factor = lax.rsqrt(first_square + 1e-06)
    correlator = jnp.stack([corr_real, corr_imag])[None]
    projected = (raw_pair * scale_factor)[None]
    return (correlator, projected)


def solution(mesh):
    placed = (
        P("ta", "gx", None, None, None),
        P("ta", None, "gx", None, None, None),
        P(),
        P(),
        P(),
        P(),
        P(),
    )
    return jax.shard_map(
        body,
        mesh=mesh,
        in_specs=placed,
        out_specs=(P("ta", None, None, None), P("ta", None, None, None)),
        check_vma=False,
    )
```

profile of v0, /device:TPU:0, one launch (start us, length us, event | category | flops | bytes accessed | tf_op | source)
XLA Modules:
  0.0 439.2 jit_solution(5919730294180601263)
XLA Ops:
  23.9 16.5 %slice_reduce_fusion = (bf16[512,3,384]{2,1,0:T(4,128)(2,1)}, bf16[512,3,384]{2,1,0:T(4,128)(2,1)}) fusion(bf16[512,3,2,384]{3,2,1,0:T(2,128)(2,1)S(1)} %bitcast.252), kind=kLoop, calls=%fused_computation.174 | loop fusion | bytes 4718592 | tf_op jit(solution)/shard_map/slice | solution.py:166
  47.9 7.6 %fusion.262 = (bf16[1536,384]{1,0:T(8,128)(2,1)S(1)}, bf16[1536,384]{1,0:T(8,128)(2,1)S(1)}, bf16[1536,384]{1,0:T(8,128)(2,1)}, bf16[1536,384]{1,0:T(8,128)(2,1)...) fusion(bf16[1536,384]{1,0:T(8,128)(2,1)S(1)} %reshape_squeeze.7, ...), kind=kLoop, calls=%fused_computation.326 | loop fusion | flops 34209792 | bytes 22511616 | tf_op jit(solution)/shard_map/neg | solution.py:123
  57.8 6.8 %fusion.131 = (bf16[1536,384]{1,0:T(8,128)(2,1)S(1)}, bf16[1536,384]{1,0:T(8,128)(2,1)}, bf16[1536,384]{1,0:T(8,128)(2,1)}, bf16[1536,384]{1,0:T(8,128)(2,1)}, b...) fusion(bf16[1536,384]{1,0:T(8,128)(2,1)S(1)} %reshape_squeeze.6, ...), kind=kLoop, calls=%fused_computation.173 | loop fusion | flops 20054016 | bytes 11894784 | tf_op jit(solution)/shard_map/convert_element_type | solution.py:120
  64.6 19.0 %fusion.64 = f32[384,768]{1,0:T(8,128)} fusion(bf16[3072,384]{1,0:T(8,128)(2,1)S(1)} %get-tuple-element.47, bf16[1536,384]{1,0:T(8,128)(2,1)S(1)} %get-tuple-element.4, bf16[1536,384]{1,0:T(8,128)(2,1)S(1)} %get-tuple-element.24, bf16[1536,384]{1,0:T(8,128)(2,1)S(1)} %get-tuple-element.5), kind=kOutput, calls=%fused_computation.100 | convolution fusion | flops 1830813696 | bytes 7077888 | tf_op jit(solution)/shard_map/dot_general | solution.py:156
  86.2 8.4 %all-to-all-start.8 = ((f32[32,12,768]{2,1,0:T(8,128)}), f32[32,12,768]{2,1,0:T(8,128)}, u32[]{:S(2)}, u32[]{:S(2)}) async-start(f32[32,12,768]{2,1,0:T(8,128)} %reshape.299), calls=%async_computation.8 | async-start | bytes 3145728 | tf_op jit(solution)/shard_map/all_to_all | solution.py:24
  101.2 16.5 %all-to-all-done.8 = f32[32,12,768]{2,1,0:T(8,128)} async-done(((f32[32,12,768]{2,1,0:T(8,128)}), f32[32,12,768]{2,1,0:T(8,128)}, u32[]{:S(2)}, u32[]{:S(2)}) %all-to-all-start.8) | async-done | bytes 1179680 | tf_op jit(solution)/shard_map/all_to_all | solution.py:24
  121.7 5.8 %fusion.48 = f32[384,768]{1,0:T(8,128)} fusion(bf16[3072,384]{1,0:T(8,128)(2,1)} %copy-done.23, bf16[1536,384]{1,0:T(8,128)(2,1)S(1)} %get-tuple-element.42, bf16[1536,384]{1,0:T(8,128)(2,1)} %get-tuple-element.31, bf16[1536,384]{1,0:T(8,128)(2,1)} %get-tuple-element.43), kind=kOutput, calls=%fused_computation.84 | convolution fusion | flops 1830813696 | bytes 7077888 | tf_op jit(solution)/shard_map/dot_general | solution.py:156
  130.0 14.8 %all-to-all-done.7 = f32[32,12,768]{2,1,0:T(8,128)S(1)} async-done(((f32[32,12,768]{2,1,0:T(8,128)}), f32[32,12,768]{2,1,0:T(8,128)S(1)}, u32[]{:S(2)}, u32[]{:S(2)}) %all-to-all-start.7) | async-done | bytes 1179680 | tf_op jit(solution)/shard_map/all_to_all | solution.py:24
  149.0 6.2 %fusion.40 = f32[384,768]{1,0:T(8,128)} fusion(bf16[3072,384]{1,0:T(8,128)(2,1)} %copy-done.23, bf16[1536,384]{1,0:T(8,128)(2,1)} %get-tuple-element.40, bf16[1536,384]{1,0:T(8,128)(2,1)} %get-tuple-element.30, bf16[1536,384]{1,0:T(8,128)(2,1)} %get-tuple-element.41), kind=kOutput, calls=%fused_computation.76 | convolution fusion | flops 1830813696 | bytes 7077888 | tf_op jit(solution)/shard_map/dot_general | solution.py:156
  157.6 14.3 %all-to-all-done.6 = f32[32,12,768]{2,1,0:T(8,128)S(1)} async-done(((f32[32,12,768]{2,1,0:T(8,128)}), f32[32,12,768]{2,1,0:T(8,128)S(1)}, u32[]{:S(2)}, u32[]{:S(2)}) %all-to-all-start.6) | async-done | bytes 1179680 | tf_op jit(solution)/shard_map/all_to_all | solution.py:24
  175.9 6.1 %fusion.32 = f32[384,768]{1,0:T(8,128)} fusion(bf16[3072,384]{1,0:T(8,128)(2,1)} %copy-done.23, bf16[1536,384]{1,0:T(8,128)(2,1)} %get-tuple-element.38, bf16[1536,384]{1,0:T(8,128)(2,1)} %get-tuple-element.29, bf16[1536,384]{1,0:T(8,128)(2,1)} %get-tuple-element.39), kind=kOutput, calls=%fused_computation.68 | convolution fusion | flops 1830813696 | bytes 7077888 | tf_op jit(solution)/shard_map/dot_general | solution.py:156
  184.4 14.6 %all-to-all-done.5 = f32[32,12,768]{2,1,0:T(8,128)S(1)} async-done(((f32[32,12,768]{2,1,0:T(8,128)}), f32[32,12,768]{2,1,0:T(8,128)S(1)}, u32[]{:S(2)}, u32[]{:S(2)}) %all-to-all-start.5) | async-done | bytes 1179680 | tf_op jit(solution)/shard_map/all_to_all | solution.py:24
  203.0 6.2 %fusion.24 = f32[384,768]{1,0:T(8,128)} fusion(bf16[3072,384]{1,0:T(8,128)(2,1)} %copy-done.23, bf16[1536,384]{1,0:T(8,128)(2,1)} %get-tuple-element.36, bf16[1536,384]{1,0:T(8,128)(2,1)} %get-tuple-element.28, bf16[1536,384]{1,0:T(8,128)(2,1)} %get-tuple-element.37), kind=kOutput, calls=%fused_computation.60 | convolution fusion | flops 1830813696 | bytes 7077888 | tf_op jit(solution)/shard_map/dot_general | solution.py:156
  211.6 14.5 %all-to-all-done.4 = f32[32,12,768]{2,1,0:T(8,128)S(1)} async-done(((f32[32,12,768]{2,1,0:T(8,128)}), f32[32,12,768]{2,1,0:T(8,128)S(1)}, u32[]{:S(2)}, u32[]{:S(2)}) %all-to-all-start.4) | async-done | bytes 1179680 | tf_op jit(solution)/shard_map/all_to_all | solution.py:24
  230.1 6.1 %fusion.16 = f32[384,768]{1,0:T(8,128)} fusion(bf16[3072,384]{1,0:T(8,128)(2,1)} %copy-done.23, bf16[1536,384]{1,0:T(8,128)(2,1)} %get-tuple-element.34, bf16[1536,384]{1,0:T(8,128)(2,1)} %get-tuple-element.27, bf16[1536,384]{1,0:T(8,128)(2,1)} %get-tuple-element.35), kind=kOutput, calls=%fused_computation.52 | convolution fusion | flops 1830813696 | bytes 7077888 | tf_op jit(solution)/shard_map/dot_general | solution.py:156
  238.6 14.6 %all-to-all-done.3 = f32[32,12,768]{2,1,0:T(8,128)S(1)} async-done(((f32[32,12,768]{2,1,0:T(8,128)}), f32[32,12,768]{2,1,0:T(8,128)S(1)}, u32[]{:S(2)}, u32[]{:S(2)}) %all-to-all-start.3) | async-done | bytes 1179680 | tf_op jit(solution)/shard_map/all_to_all | solution.py:24
  257.5 6.1 %fusion.8 = f32[384,768]{1,0:T(8,128)} fusion(bf16[3072,384]{1,0:T(8,128)(2,1)} %copy-done.23, bf16[1536,384]{1,0:T(8,128)(2,1)} %get-tuple-element.32, bf16[1536,384]{1,0:T(8,128)(2,1)} %get-tuple-element.26, bf16[1536,384]{1,0:T(8,128)(2,1)} %get-tuple-element.33), kind=kOutput, calls=%fused_computation.44 | convolution fusion | flops 1830813696 | bytes 7077888 | tf_op jit(solution)/shard_map/dot_general | solution.py:156
  271.7 9.0 %all-to-all-done.2 = f32[32,12,768]{2,1,0:T(8,128)S(1)} async-done(((f32[32,12,768]{2,1,0:T(8,128)}), f32[32,12,768]{2,1,0:T(8,128)S(1)}, u32[]{:S(2)}, u32[]{:S(2)}) %all-to-all-start.2) | async-done | bytes 1179680 | tf_op jit(solution)/shard_map/all_to_all | solution.py:24
  291.9 16.6 %all-to-all-done.1 = f32[32,12,768]{2,1,0:T(8,128)} async-done(((f32[32,12,768]{2,1,0:T(8,128)}), f32[32,12,768]{2,1,0:T(8,128)}, u32[]{:S(2)}, u32[]{:S(2)}) %all-to-all-start.1) | async-done | bytes 1179680 | tf_op jit(solution)/shard_map/all_to_all | solution.py:24
  330.4 5.9 %all-to-all-done = f32[32,12,768]{2,1,0:T(8,128)} async-done(((f32[32,12,768]{2,1,0:T(8,128)}), f32[32,12,768]{2,1,0:T(8,128)}, u32[]{:S(2)}, u32[]{:S(2)}) %all-to-all-start) | async-done | bytes 1179680 | tf_op jit(solution)/shard_map/all_to_all | solution.py:24
  338.0 10.6 %fusion.280 = (bf16[1,1,384,4,4,384]{5,4,3,1,0,2:T(4,128)(2,1)}, bf16[1,1,384,4,4,384]{5,4,3,1,0,2:T(4,128)(2,1)}) fusion(bf16[1,2,384,4,4,384]{5,4,3,1,0,2:T(4,128)(2,1)} %all-gather.2.cloned.1.call-done), kind=kLoop, calls=%fused_computation.335 | loop fusion | bytes 18874368 | tf_op jit(solution)/shard_map/slice | solution.py:181
  368.2 5.5 %fusion.136 = f32[9,4,4,9,4,4]{0,3,2,1,4,5:T(8,128)S(1)} fusion(f32[4,4,9,9,4,4,1]{3,2,6,5,4,1,0:T(8,128)S(1)} %fusion.84, bf16[9,12,4,4,384,1,1]{4,1,3,2,0,6,5:T(8,128)(2,1)S(1)} %fusion.160, bf16[12,4,4,9,384,1,1]{4,0,3,2,1,6,5:T(8,128)(2,1)S(1)} %copy-done.18), kind=kOutput, calls=%fused_computation.181 | convolution fusion | flops 191123712 | bytes 2820096 | tf_op jit(solution)/shard_map/mrxyk,rawnk->mxynwa/dot_general | solution.py:85
  399.4 16.2 %all-to-all-done.9 = f32[32,1,8192]{2,1,0:T(1,128)S(1)} async-done(((f32[32,1,8192]{2,1,0:T(1,128)}), f32[32,1,8192]{2,1,0:T(1,128)S(1)}, u32[]{:S(2)}, u32[]{:S(2)}) %all-to-all-start.9) | async-done | bytes 1048608 | tf_op jit(solution)/shard_map/all_to_all | solution.py:30
  420.0 10.8 %all-reduce = f32[4]{0:T(128)S(1)} all-reduce(f32[4]{0:T(128)S(1)} %dynamic-update-slice), channel_id=1, replica_groups=mesh['ta'=4,'gx'=32] {'ta'}, use_global_device_ids=true, to_apply=%add | all-reduce | flops 4 | bytes 32
  (253 shorter events, 164.7 us)
Async XLA Ops:
  7.2 330.8 %all-gather.2.cloned.1.call-start = ((), (), s32[]{:S(2)}) async-start(), calls=%async_computation.10 | async-start | bytes 9732096 | tf_op jit(solution)/shard_map/all_gather | solution.py:179
  47.9 7.6 %copy-start.39 = (f32[1536]{0:T(1024)S(1)}, f32[1536]{0:T(1024)}, u32[]{:S(2)}) copy-start(f32[1536]{0:T(1024)} %mul.559) | copy-start | bytes 18436
  47.9 7.6 %copy-start.40 = (f32[1536]{0:T(1024)S(1)}, f32[1536]{0:T(1024)}, u32[]{:S(2)}) copy-start(f32[1536]{0:T(1024)} %mul.564) | copy-start | bytes 18436
  86.2 31.6 %all-to-all-start.8 = ((f32[32,12,768]{2,1,0:T(8,128)}), f32[32,12,768]{2,1,0:T(8,128)}, u32[]{:S(2)}, u32[]{:S(2)}) async-start(f32[32,12,768]{2,1,0:T(8,128)} %reshape.299), calls=%async_computation.8 | async-start | bytes 3145728 | tf_op jit(solution)/shard_map/all_to_all | solution.py:24
  117.7 27.1 %all-to-all-start.7 = ((f32[32,12,768]{2,1,0:T(8,128)}), f32[32,12,768]{2,1,0:T(8,128)S(1)}, u32[]{:S(2)}, u32[]{:S(2)}) async-start(f32[32,12,768]{2,1,0:T(8,128)} %reshape.298), calls=%async_computation.7 | async-start | bytes 3145728 | tf_op jit(solution)/shard_map/all_to_all | solution.py:24
  144.8 10.4 %copy-start.1 = (f32[32,12,768]{2,1,0:T(8,128)}, f32[32,12,768]{2,1,0:T(8,128)S(1)}, u32[]{:S(2)}) copy-start(f32[32,12,768]{2,1,0:T(8,128)S(1)} %all-to-all-done.7) | copy-start | bytes 3538948
  144.8 27.1 %all-to-all-start.6 = ((f32[32,12,768]{2,1,0:T(8,128)}), f32[32,12,768]{2,1,0:T(8,128)S(1)}, u32[]{:S(2)}, u32[]{:S(2)}) async-start(f32[32,12,768]{2,1,0:T(8,128)} %reshape.297), calls=%async_computation.6 | async-start | bytes 3145728 | tf_op jit(solution)/shard_map/all_to_all | solution.py:24
  171.9 10.1 %copy-start.3 = (f32[32,12,768]{2,1,0:T(8,128)}, f32[32,12,768]{2,1,0:T(8,128)S(1)}, u32[]{:S(2)}) copy-start(f32[32,12,768]{2,1,0:T(8,128)S(1)} %all-to-all-done.6) | copy-start | bytes 3538948
  171.9 27.1 %all-to-all-start.5 = ((f32[32,12,768]{2,1,0:T(8,128)}), f32[32,12,768]{2,1,0:T(8,128)S(1)}, u32[]{:S(2)}, u32[]{:S(2)}) async-start(f32[32,12,768]{2,1,0:T(8,128)} %reshape.296), calls=%async_computation.5 | async-start | bytes 3145728 | tf_op jit(solution)/shard_map/all_to_all | solution.py:24
  199.0 10.2 %copy-start.5 = (f32[32,12,768]{2,1,0:T(8,128)}, f32[32,12,768]{2,1,0:T(8,128)S(1)}, u32[]{:S(2)}) copy-start(f32[32,12,768]{2,1,0:T(8,128)S(1)} %all-to-all-done.5) | copy-start | bytes 3538948
  199.0 27.1 %all-to-all-start.4 = ((f32[32,12,768]{2,1,0:T(8,128)}), f32[32,12,768]{2,1,0:T(8,128)S(1)}, u32[]{:S(2)}, u32[]{:S(2)}) async-start(f32[32,12,768]{2,1,0:T(8,128)} %reshape.295), calls=%async_computation.4 | async-start | bytes 3145728 | tf_op jit(solution)/shard_map/all_to_all | solution.py:24
  226.1 10.1 %copy-start.7 = (f32[32,12,768]{2,1,0:T(8,128)}, f32[32,12,768]{2,1,0:T(8,128)S(1)}, u32[]{:S(2)}) copy-start(f32[32,12,768]{2,1,0:T(8,128)S(1)} %all-to-all-done.4) | copy-start | bytes 3538948
  226.1 27.1 %all-to-all-start.3 = ((f32[32,12,768]{2,1,0:T(8,128)}), f32[32,12,768]{2,1,0:T(8,128)S(1)}, u32[]{:S(2)}, u32[]{:S(2)}) async-start(f32[32,12,768]{2,1,0:T(8,128)} %reshape.294), calls=%async_computation.3 | async-start | bytes 3145728 | tf_op jit(solution)/shard_map/all_to_all | solution.py:24
  253.2 10.5 %copy-start.9 = (f32[32,12,768]{2,1,0:T(8,128)}, f32[32,12,768]{2,1,0:T(8,128)S(1)}, u32[]{:S(2)}) copy-start(f32[32,12,768]{2,1,0:T(8,128)S(1)} %all-to-all-done.3) | copy-start | bytes 3538948
  253.2 27.5 %all-to-all-start.2 = ((f32[32,12,768]{2,1,0:T(8,128)}), f32[32,12,768]{2,1,0:T(8,128)S(1)}, u32[]{:S(2)}, u32[]{:S(2)}) async-start(f32[32,12,768]{2,1,0:T(8,128)} %reshape.293), calls=%async_computation.2 | async-start | bytes 3145728 | tf_op jit(solution)/shard_map/all_to_all | solution.py:24
  271.6 13.8 %copy-start.46 = (s32[64]{0:T(128)S(1)}, s32[64]{0:T(128)}, u32[]{:S(2)}) copy-start(s32[64]{0:T(128)} %param.14) | copy-start | bytes 772
  271.6 15.1 %copy-start.42 = (f32[16,16]{0,1:T(8,128)S(1)}, f32[16,16]{0,1:T(8,128)}, u32[]{:S(2)}) copy-start(f32[16,16]{0,1:T(8,128)} %constant.75) | copy-start | bytes 3076
  271.6 15.2 %copy-start.45 = (f32[4]{0:T(128)S(1)}, f32[4]{0:T(128)}, u32[]{:S(2)}) copy-start(f32[4]{0:T(128)} %constant.65.clone) | copy-start | bytes 52
  271.7 15.9 %copy-start.21 = (bf16[1,2,12,4,4,384]{5,4,3,2,1,0:T(4,128)(2,1)S(1)}, bf16[1,2,12,4,4,384]{5,4,3,2,1,0:T(4,128)(2,1)}, u32[]{:S(2)}) copy-start(bf16[1,2,12,4,4,384]{5,4,3,2,1,0:T(4,128)(2,1)} %param.11) | copy-start | bytes 884740
  280.7 27.8 %all-to-all-start.1 = ((f32[32,12,768]{2,1,0:T(8,128)}), f32[32,12,768]{2,1,0:T(8,128)}, u32[]{:S(2)}, u32[]{:S(2)}) async-start(f32[32,12,768]{2,1,0:T(8,128)} %reshape.292), calls=%async_computation.1 | async-start | bytes 3145728 | tf_op jit(solution)/shard_map/all_to_all | solution.py:24
  308.5 27.8 %all-to-all-start = ((f32[32,12,768]{2,1,0:T(8,128)}), f32[32,12,768]{2,1,0:T(8,128)}, u32[]{:S(2)}, u32[]{:S(2)}) async-start(f32[32,12,768]{2,1,0:T(8,128)} %reshape.291), calls=%async_computation | async-start | bytes 3145728 | tf_op jit(solution)/shard_map/all_to_all | solution.py:24
  391.2 7.6 %copy-start.47 = (u32[128]{0:T(128)S(1)}, u32[128]{0:T(128)}, u32[]{:S(2)}) copy-start(u32[128]{0:T(128)} %constant.70) | copy-start | bytes 1540
  392.5 23.9 %copy-start.24 = (f32[2,64,8]{1,2,0:T(8,128)S(1)}, f32[2,64,8]{1,2,0:T(8,128)}, u32[]{:S(2)}) copy-start(f32[2,64,8]{1,2,0:T(8,128)} %param.16) | copy-start | bytes 12292
  394.9 20.7 %all-to-all-start.9 = ((f32[32,1,8192]{2,1,0:T(1,128)}), f32[32,1,8192]{2,1,0:T(1,128)S(1)}, u32[]{:S(2)}, u32[]{:S(2)}) async-start(f32[32,1,8192]{2,1,0:T(1,128)} %broadcast_in_dim.4), calls=%async_computation.9 | async-start | bytes 2097152 | tf_op jit(solution)/shard_map/all_to_all | solution.py:30
  (39 other events, 118.9 us)
Sparse Core Ops, SparseCore 0:
  10.2 57.9 all-gather.1
where the time goes:
time: 445 us; the launch traced here: 439 us
  waiting for transfers between devices  137 us (31%)
  matrix products  123 us (28%)
  local copies, waits for them, and re-layouts  80.7 us (18%)
  starting transfers between devices  46.4 us (10%)
  other arithmetic  25.9 us (6%)
  between operations  15.9 us (4%)
  blocking collectives  10.8 us (2%)
    all_to_all x9, waiting for transfers between devices, sent_and_summed(): lax.all_to_all(cut_along(shard, dim, length), axis, 0, 0, tiled=True)  121 us
    dot_general x9, matrix products, transpose_product(): lax.dot_general(conj_left, twist_right, (((0,), (0,)), ((), ())), preferr...  64.5 us
    dot_general x28, matrix products, single(): jnp.einsum(form, left_part, right_part, precision=full_precision, preferr...  57.9 us
    all_to_all x9, starting transfers between devices, sent_and_summed(): lax.all_to_all(cut_along(shard, dim, length), axis, 0, 0, tiled=True)  42.5 us
    reshape x9, local copies, waits for them, and re-layouts, cut_along(): shard.reshape(*dims[:dim], length, dims[dim] // length, *dims[dim + 1:])  19.9 us
    slice x1, local copies, waits for them, and re-layouts, body(): vec_imag = vectors[:, :, 1, :]  16.5 us
    all_to_all x1, waiting for transfers between devices, from_everyone(): lax.all_to_all(jnp.broadcast_to(shard[None], (length, *shard.shape)), axi...  16.2 us
    unnamed x1, blocking collectives  10.8 us
  transfers between devices with their start and end apart: 11, of which 10 were waited for; matrix products, arithmetic and copies ran while one was open for 37% of the time, Pallas kernels for 0%

commit v1 on v0

v1 whole, which is shorter than its diff:
```python
import functools
import math

import jax
import jax.numpy as jnp
import numpy as np
from jax import lax
from jax.experimental import pallas as pl
from jax.experimental.pallas import tpu as pltpu
from jax.sharding import PartitionSpec as P

EXTENT = 96
NMOM = 9
BF = jnp.bfloat16
F32 = jnp.float32
HALF_PERIOD = -2.0 * math.pi / EXTENT
CHUNK = 768
ROWS = 24
MPAD = 16
VMEM = 60 << 20
full_precision = lax.Precision.HIGHEST
SAME_CORE = [[d for d in range(32) if d % 2 == c] for c in range(2)]
PAIR = [(d, d ^ 1) for d in range(32)]


def gamma_tables():
    zero_block = np.zeros((4, 4), np.float32)
    first_imag = np.array([[0, 0, 0, 1], [0, 0, 1, 0], [0, -1, 0, 0], [-1, 0, 0, 0]], np.float32)
    second_real = np.array([[0, 0, 0, -1], [0, 0, 1, 0], [0, 1, 0, 0], [-1, 0, 0, 0]], np.float32)
    third_imag = np.array([[0, 0, 1, 0], [0, 0, 0, -1], [-1, 0, 0, 0], [0, 1, 0, 0]], np.float32)
    fourth_real = np.array([[0, 0, 1, 0], [0, 0, 0, 1], [1, 0, 0, 0], [0, 1, 0, 0]], np.float32)
    gamma_list = [
        (zero_block, first_imag),
        (second_real, zero_block),
        (zero_block, third_imag),
        (fourth_real, zero_block),
    ]
    real_parts = []
    imag_parts = []
    for subset in range(16):
        prod_real = np.eye(4, dtype=np.float32)
        prod_imag = np.zeros((4, 4), np.float32)
        for position in range(4):
            if subset >> position & 1:
                factor_real, factor_imag = gamma_list[position]
                prod_real, prod_imag = (
                    prod_real @ factor_real - prod_imag @ factor_imag,
                    prod_real @ factor_imag + prod_imag @ factor_real,
                )
        real_parts.append(prod_real)
        imag_parts.append(prod_imag)
    return (np.stack(real_parts).astype(np.float32), np.stack(imag_parts).astype(np.float32))


def spin_tables():
    chiral = np.array([1.0, 1.0, -1.0, -1.0], np.float32)
    parts = np.stack(gamma_tables())
    left = np.transpose(parts, (0, 2, 1, 3)) * chiral[None, :, None, None]
    left = np.repeat(left[..., None], MPAD, -1).reshape(2, 4, 16, 4 * MPAD)
    right = np.transpose(parts, (0, 3, 1, 2)) * chiral
    right = right * np.array([1.0, -1.0], np.float32)[:, None, None, None]
    right = np.broadcast_to(right[:, :, :, None, None, :], (2, 4, 16, NMOM, 4, 4))
    return left, right.reshape(2, 4, 16, NMOM * 16)


def dot(left, right, lc, rc, precision=None):
    return lax.dot_general(
        left, right, (((lc,), (rc,)), ((), ())), precision=precision, preferred_element_type=F32
    )


def phase_kernel(first, full, half, steps, where_ref, mom_ref, own_ref, other_ref, out_ref, acc_ref):
    step = pl.program_id(0)
    core = lax.rem(where_ref[0], 2)
    is_own = step < steps
    real = jnp.where(is_own, own_ref[0], other_ref[0])
    imag = jnp.where(is_own, own_ref[1], other_ref[1])
    left = jnp.concatenate([real.T, imag.T], 1)
    device = jnp.where(is_own, where_ref[0], where_ref[0] + 1 - 2 * core)
    unit = lax.broadcasted_iota(jnp.int32, (8, CHUNK), 0)
    row = lax.rem(step, steps) * CHUNK + lax.broadcasted_iota(jnp.int32, (8, CHUNK), 1)
    site = jnp.floor((row.astype(F32) + 0.5) * (1.0 / 3.0)) + (device * 512).astype(F32)
    line = jnp.floor((site + 0.5) * (1.0 / EXTENT))
    xcoord = site - EXTENT * line
    zcoord = jnp.floor((line + 0.5) * (1.0 / EXTENT))
    ycoord = line - EXTENT * zcoord
    winding = jnp.zeros((8, CHUNK), F32)
    for u in range(full + half):
        m = 4 * core + first + u if u < full else NMOM - 1
        here = (
            mom_ref[3 * m].astype(F32) * xcoord
            + mom_ref[3 * m + 1].astype(F32) * ycoord
            + mom_ref[3 * m + 2].astype(F32) * zcoord
        )
        winding = jnp.where(unit == u, here, winding)
    winding = winding - EXTENT * jnp.floor((winding + 0.5) * (1.0 / EXTENT))
    angle = winding * HALF_PERIOD
    cosine = jnp.cos(angle)
    sine = jnp.sin(angle)
    if half:
        turned = jnp.logical_and(unit == full, core == 1)
        cosine, sine = jnp.where(turned, sine, cosine), jnp.where(turned, -cosine, sine)
    cosine = cosine.T
    sine = sine.T
    real = real.astype(F32)
    imag = imag.astype(F32)

    @pl.when(step == 0)
    def _():
        acc_ref[...] = jnp.zeros_like(acc_ref)

    for u in range(full + half):
        c = cosine[:, u : u + 1]
        s = sine[:, u : u + 1]
        twist_real = (c * real - s * imag).astype(BF)
        twist_imag = (c * imag + s * real).astype(BF)
        if u < full:
            right = jnp.concatenate(
                [
                    jnp.concatenate([twist_real, twist_imag], 1),
                    jnp.concatenate([twist_imag, -twist_real], 1),
                ],
                0,
            )
        else:
            right = jnp.concatenate([twist_real, twist_imag], 0)
        at = slice(768 * u, 768 * u + right.shape[1])
        acc_ref[:, at] += dot(left, right, 1, 0)

    @pl.when(step == 2 * steps - 1)
    def _():
        for j in range(16):
            out_ref[j] = acc_ref[ROWS * j : ROWS * (j + 1), :].astype(BF)


def phase_part(own, other, where, momenta, first, full, half):
    steps = own.shape[1] // CHUNK
    width = 768 * full + 384 * half
    return pl.pallas_call(
        functools.partial(phase_kernel, first, full, half, steps),
        grid_spec=pltpu.PrefetchScalarGridSpec(
            num_scalar_prefetch=2,
            grid=(2 * steps,),
            in_specs=[
                pl.BlockSpec((2, CHUNK, 384), lambda c, *_: (0, jnp.minimum(c, steps - 1), 0)),
                pl.BlockSpec((2, CHUNK, 384), lambda c, *_: (0, jnp.maximum(c - steps, 0), 0)),
            ],
            out_specs=pl.BlockSpec((16, ROWS, width), lambda c, *_: (0, 0, 0)),
            scratch_shapes=[pltpu.VMEM((384, width), F32)],
        ),
        out_shape=jax.ShapeDtypeStruct((16, ROWS, width), BF),
        compiler_params=pltpu.CompilerParams(vmem_limit_bytes=VMEM),
        name=f"phase_{first}",
    )(where, momenta, own, other)


def source_kernel(
    where_ref, tau_ref, src_ref, mom_ref, gam_ref, ltab_ref, rtab_ref, out_ref, left_ref, right_ref
):
    n = pl.program_id(0)
    x = jnp.concatenate([tau_ref[:, 0].reshape(384, 384), tau_ref[:, 1].reshape(384, 384)], 1)
    s_real = src_ref[0, 0]
    s_imag = src_ref[0, 1]
    to_real = jnp.concatenate([s_real, s_imag], 1)
    to_imag = jnp.concatenate([s_imag, -s_real], 1)
    out_ref[:, 0, 0] = dot(x, to_real, 1, 1).astype(BF).reshape(ROWS, 16, 192)
    out_ref[:, 1, 0] = dot(x, to_imag, 1, 1).astype(BF).reshape(ROWS, 16, 192)

    @pl.when(n == 0)
    def _():
        chosen = (gam_ref[...] == lax.broadcasted_iota(jnp.int32, (64, 16), 1)).astype(BF)
        lane = lax.rem(lax.broadcasted_iota(jnp.int32, (64, 64), 1), MPAD)
        moment = mom_ref[...] == lane
        for a in range(4):
            for q in range(2):
                got = jnp.where(moment, dot(chosen, ltab_ref[q, a], 1, 0), 0.0)
                left_ref[q, 64 * a : 64 * a + 64, :] = got
        lane = lax.broadcasted_iota(jnp.int32, (64, 144), 1)
        low = mom_ref[...] * 16
        moment = jnp.logical_and(lane >= low, lane < low + 16)
        for y in range(4):
            for q in range(2):
                right_ref[q, y] = jnp.where(moment, dot(chosen, rtab_ref[q, y], 1, 0), 0.0)


def source_part(tau, source_blocks, op_momentum, op_gamma, where):
    ltab, rtab = spin_tables()
    whole = lambda shape: pl.BlockSpec(shape, lambda n, *_: (0,) * len(shape))
    return pl.pallas_call(
        source_kernel,
        grid_spec=pltpu.PrefetchScalarGridSpec(
            num_scalar_prefetch=1,
            grid=(NMOM,),
            in_specs=[
                whole((ROWS, 2, 16, 384)),
                pl.BlockSpec((1, 2, 192, 384), lambda n, w: (n, 0, lax.rem(w[0], 2), 0)),
                whole((64, 1)),
                whole((64, 1)),
                whole((2, 4, 16, 64)),
                whole((2, 4, 16, 144)),
            ],
            out_specs=[
                pl.BlockSpec((ROWS, 2, 1, 16, 192), lambda n, *_: (0, 0, n, 0, 0)),
                whole((2, 256, 64)),
                whole((2, 4, 64, 144)),
            ],
        ),
        out_shape=[
            jax.ShapeDtypeStruct((ROWS, 2, NMOM, 16, 192), BF),
            jax.ShapeDtypeStruct((2, 256, 64), F32),
            jax.ShapeDtypeStruct((2, 4, 64, 144), F32),
        ],
        compiler_params=pltpu.CompilerParams(vmem_limit_bytes=VMEM),
        name="source",
    )(
        where,
        tau,
        source_blocks,
        op_momentum[:, None],
        op_gamma[:, None],
        jnp.asarray(ltab, BF),
        jnp.asarray(rtab, BF),
    )


def sink_kernel(
    where_ref, own1, oth1, own2, oth2, tau_ref, src_ref, left_ref, right_ref, out_ref,
    rows_ref, sink_ref, acc_ref,
):
    core = lax.rem(where_ref[0], 2)
    rows_ref[...] = jnp.zeros_like(rows_ref)
    for c in range(2):
        one = jnp.where(core == c, own1[...], oth1[...]).astype(F32)
        two = jnp.where(core == c, own2[...], oth2[...]).astype(F32)
        for u in range(4):
            part = one if u < 2 else two
            for q in range(2):
                at = 768 * (u % 2) + 384 * q
                rows_ref[q, :, 4 * c + u, :] = part[:, at : at + 384]
        rows_ref[c, :, 8, :] = two[:, 1536:1920]
    real = rows_ref[0].reshape(384, 384).astype(BF)
    imag = rows_ref[1].reshape(384, 384).astype(BF)
    stacked = jnp.concatenate(
        [jnp.concatenate([real, -imag], 1), jnp.concatenate([imag, real], 1)], 0
    )
    for g in range(4):
        at = slice(768 * g, 768 * g + 768)
        here = jnp.concatenate([tau_ref[:, at], tau_ref[:, 3072 + 768 * g : 3840 + 768 * g]], 0)
        got = dot(stacked, here, 1, 0).astype(BF)
        for y in range(4):
            for q in range(2):
                sink_ref[q, 4 * y + g] = got[384 * q : 384 * q + 384, 192 * y : 192 * y + 192]
    acc_ref[...] = jnp.zeros_like(acc_ref)

    def one_row(r, carry):
        at = pl.ds(pl.multiple_of(r * MPAD, MPAD), MPAD)
        left = jnp.concatenate([sink_ref[q, :, at, :].reshape(256, 192) for q in range(2)], 0)
        right = src_ref[r].reshape(288, 192)
        acc_ref[...] += dot(left, right, 1, 1)
        return carry

    lax.fori_loop(0, ROWS, one_row, 0)
    acc = acc_ref[...]
    block_real = acc[:256, :144] - acc[256:, 144:]
    block_imag = acc[:256, 144:] + acc[256:, :144]
    l_real = left_ref[0]
    l_imag = left_ref[1]
    lifted = jnp.concatenate(
        [jnp.concatenate([l_real, -l_imag], 1), jnp.concatenate([l_imag, l_real], 1)], 0
    )
    spin = lax.rem(lax.broadcasted_iota(jnp.int32, (64, 144), 1), 16) // 4
    corr_real = jnp.zeros((64, 64), F32)
    corr_imag = jnp.zeros((64, 64), F32)
    for y in range(4):
        at = slice(64 * y, 64 * y + 64)
        both = jnp.concatenate([block_real[at], block_imag[at]], 0)
        got = dot(lifted, both, 1, 0, full_precision)
        halves = []
        for q in range(2):
            total = jnp.zeros((64, 144), F32)
            for a in range(4):
                low = 256 * q + 64 * a
                total = jnp.where(spin == a, got[low : low + 64], total)
            halves.append(total)
        r_real = right_ref[0, y]
        r_imag = right_ref[1, y]
        corr_real += dot(halves[0], r_real, 1, 1, full_precision)
        corr_real -= dot(halves[1], r_imag, 1, 1, full_precision)
        corr_imag += dot(halves[0], r_imag, 1, 1, full_precision)
        corr_imag += dot(halves[1], r_real, 1, 1, full_precision)
    out_ref[0] = corr_real
    out_ref[1] = corr_imag


def sink_part(where, own1, oth1, own2, oth2, tau, src, left, right):
    specs = [pl.BlockSpec(memory_space=pltpu.VMEM)] * 8
    return pl.pallas_call(
        sink_kernel,
        grid_spec=pltpu.PrefetchScalarGridSpec(
            num_scalar_prefetch=1,
            grid=(),
            in_specs=specs,
            out_specs=pl.BlockSpec(memory_space=pltpu.VMEM),
            scratch_shapes=[
                pltpu.VMEM((2, ROWS, MPAD, 384), F32),
                pltpu.VMEM((2, 16, 384, 192), BF),
                pltpu.VMEM((512, 288), F32),
            ],
        ),
        out_shape=jax.ShapeDtypeStruct((2, 64, 64), F32),
        compiler_params=pltpu.CompilerParams(vmem_limit_bytes=VMEM),
        name="sink",
    )(where, own1, oth1, own2, oth2, tau, src, left, right)


def complex_einsum(form, left_real, left_imag, right_real, right_imag):

    def single(left_part, right_part):
        return jnp.einsum(
            form,
            left_part,
            right_part,
            precision=full_precision,
            preferred_element_type=jnp.float32,
        )

    return (
        single(left_real, right_real) - single(left_imag, right_imag),
        single(left_real, right_imag) + single(left_imag, right_real),
    )


def project(corr_real, corr_imag, ref_vectors):
    basis_real = ref_vectors[0]
    basis_imag = ref_vectors[1]
    half_real, half_imag = complex_einsum("ij,jv->iv", corr_real, corr_imag, basis_real, basis_imag)
    return complex_einsum("iu,iv->uv", basis_real, -basis_imag, half_real, half_imag)


def taken_together(shard, axis):
    length = lax.axis_size(axis)
    spread = jnp.broadcast_to(shard[None], (length, *shard.shape))
    return jnp.sum(lax.all_to_all(spread, axis, 0, 0, tiled=True), axis=0)


def picked(shard, axis, root):
    return lax.dynamic_index_in_dim(lax.all_gather(shard, axis), root, 0, keepdims=False)


def scattered(part):
    got = lax.all_to_all(part, "gx", 0, 0, tiled=True, axis_index_groups=SAME_CORE)
    return jnp.sum(got.astype(F32), 0).astype(BF)


def body(eigvecs, perambulators, source_blocks, momenta, op_momentum, op_gamma, ref_vectors):
    device = lax.axis_index("gx")
    core = device % 2
    where = device[None]
    own = jnp.transpose(eigvecs.reshape(-1, 2, 384), (1, 0, 2))
    other = lax.ppermute(own, "gx", PAIR)
    mine = jnp.transpose(perambulators[0], (1, 0, 2, 3, 4)).reshape(12, 2, 16, 384)
    theirs = lax.ppermute(mine, "gx", PAIR)
    tau = jnp.where(
        core == 0, jnp.concatenate([mine, theirs], 0), jnp.concatenate([theirs, mine], 0)
    )
    part = jnp.where(core == 0, tau[..., :192], tau[..., 192:]).reshape(ROWS, 6144)
    tau_all = lax.all_gather(part, "gx", axis=0, tiled=True, axis_index_groups=SAME_CORE)
    flat = momenta.reshape(-1)
    first = phase_part(own, other, where, flat, 0, 2, 0)
    own1 = scattered(first)
    second = phase_part(own, other, where, flat, 2, 2, 1)
    own2 = scattered(second)
    oth1 = lax.ppermute(own1, "gx", PAIR)
    oth2 = lax.ppermute(own2, "gx", PAIR)
    src, left, right = source_part(tau, source_blocks, op_momentum, op_gamma, where)
    corr = sink_part(where, own1, oth1, own2, oth2, tau_all, src, left, right)
    corr = taken_together(corr.reshape(-1), "gx").reshape(2, 64, 64)
    proj_real, proj_imag = project(corr[0], corr[1], ref_vectors)
    raw_pair = jnp.stack([proj_real, proj_imag])
    local_square = jnp.mean(raw_pair * raw_pair)
    first_square = picked(local_square, "ta", 0)
    scale_factor = lax.rsqrt(first_square + 1e-06)
    return (corr[None], (raw_pair * scale_factor)[None])


def solution(mesh):
    placed = (
        P("ta", "gx", None, None, None),
        P("ta", None, "gx", None, None, None),
        P(),
        P(),
        P(),
        P(),
        P(),
    )
    return jax.shard_map(
        body,
        mesh=mesh,
        in_specs=placed,
        out_specs=(P("ta", None, None, None), P("ta", None, None, None)),
        check_vma=False,
    )
```

time: 445 us -> 182 us (0.41); the launches traced: 439 us -> 181 us
  matrix products: 123 us -> 1.23 us
  waiting for transfers between devices: 137 us -> 55.3 us
  local copies, waits for them, and re-layouts: 80.7 us -> 12.4 us
  Pallas kernels: 0 us -> 62.9 us
  starting transfers between devices: 46.4 us -> 20.2 us
  other arithmetic: 25.9 us -> 2.57 us
    all_to_all x10 -> x3, waiting for transfers between devices: 137 us -> 50.2 us  [the longest x2 34 us: scattered(): lax.all_to_all(part, 'gx', 0, 0, tiled=True, axis_index_groups=SAME_CORE)]
    dot_general x9 -> x0, matrix products: 64.5 us -> none  [transpose_product(): lax.dot_general(conj_left, twist_right, (((0,), (0,)), ((), ())), preferr...]
    pallas_call x0 -> x4, Pallas kernels: none -> 62.9 us  [the longest x2 32.7 us: phase_part(): pl.pallas_call(functools.partial(phase_kernel, first, full, half, steps),...]
    dot_general x28 -> x8, matrix products: 57.9 us -> 1.23 us  [single(): jnp.einsum(form, left_part, right_part, precision=full_precision, preferr...]
    slice x8 -> x3, local copies, waits for them, and re-layouts: 28.1 us -> 0.15 us  [body(): proj_real, proj_imag = project(corr[0], corr[1], ref_vectors)]
    all_to_all x10 -> x3, starting transfers between devices: 46.4 us -> 19.6 us  [the longest x2 15.5 us: scattered(): lax.all_to_all(part, 'gx', 0, 0, tiled=True, axis_index_groups=SAME_CORE)]
    mul x37 -> x0, local copies, waits for them, and re-layouts: 16.4 us -> none  [the longest x18 7.79 us: right_block(): sine_row * vec_imag]
    reshape x11 -> x5, local copies, waits for them, and re-layouts: 20 us -> 5.03 us  [the longest x1 1.97 us: body(): own = jnp.transpose(eigvecs.reshape(-1, 2, 384), (1, 0, 2))]
  transfers between devices with their start and end apart: 11 -> 8, of which waited for: 10 -> 5; matrix products, arithmetic and copies ran while one was open for 37% -> 3% of each run, Pallas kernels for 0% -> 23%
where the time goes in v1:
time: 182 us; the launch traced here: 181 us
  Pallas kernels  62.9 us (35%)
  waiting for transfers between devices  55.3 us (30%)
  starting transfers between devices  20.2 us (11%)
  between operations  15 us (8%)
  local copies, waits for them, and re-layouts  12.4 us (7%)
  blocking collectives  11.4 us (6%)
  other arithmetic  2.57 us (1%)
    all_to_all x2, waiting for transfers between devices, scattered(): lax.all_to_all(part, 'gx', 0, 0, tiled=True, axis_index_groups=SAME_CORE)  34 us
    pallas_call x2, Pallas kernels, phase_part(): pl.pallas_call(functools.partial(phase_kernel, first, full, half, steps),...  32.7 us
    pallas_call x1, Pallas kernels, sink_part(): pl.pallas_call(sink_kernel, grid_spec=pltpu.PrefetchScalarGridSpec(num_sc...  20.6 us
    all_to_all x1, waiting for transfers between devices, taken_together(): return jnp.sum(lax.all_to_all(spread, axis, 0, 0, tiled=True), axis=0)  16.2 us
    all_to_all x2, starting transfers between devices, scattered(): lax.all_to_all(part, 'gx', 0, 0, tiled=True, axis_index_groups=SAME_CORE)  15.5 us
    unnamed x1, blocking collectives  11.4 us
    pallas_call x1, Pallas kernels, source_part(): pl.pallas_call(source_kernel, grid_spec=pltpu.PrefetchScalarGridSpec(num_...  9.52 us
    all_to_all x1, starting transfers between devices, taken_together(): return jnp.sum(lax.all_to_all(spread, axis, 0, 0, tiled=True), axis=0)  4.06 us
  transfers between devices with their start and end apart: 8, of which 5 were waited for; matrix products, arithmetic and copies ran while one was open for 3% of the time, Pallas kernels for 23%

profile of v1, /device:TPU:0, one launch (start us, length us, event | category | flops | bytes accessed | tf_op | source)
XLA Modules:
  0.0 181.0 jit_solution(10929963453187395482)
XLA Ops:
  7.2 1.0 reshape.88
  8.4 1.6 collective-permute-done.3
  10.2 1.1 reshape.82
  11.4 2.0 %copy.53 = bf16[1536,2,384]{2,0,1:T(8,128)(2,1)S(1)} copy(bf16[1536,2,384]{2,1,0:T(2,128)(2,1)} %bitcast.54) | data formatting | bytes 4718592 | tf_op jit(solution)/shard_map/reshape | solution.py:359
  13.7 0.9 reshape.79.mom_ref
  14.6 3.6 %collective-permute-done.other_ref = bf16[2,1536,384]{2,1,0:T(8,128)(2,1)} collective-permute-done((bf16[2,1536,384]{2,1,0:T(8,128)(2,1)S(1)}, bf16[2,1536,384]{2,1,0:T(8,128)(2,1)}, u32[]{:S(2)}, u32[]{:S(2)}) %collective-permute-start) | collective-permute-done | bytes 2359328 | tf_op jit(solution)/shard_map/ppermute | solution.py:360
  18.1 17.5 %phase_2.1 = bf16[16,24,1920]{2,1,0:T(8,128)(2,1)} custom-call(s32[1]{0:T(128)} %bitcast.where_ref, s32[27]{0:T(128)} %reshape.79.mom_ref, bf16[2,1536,384]{2,1,0:T(8,128)(2,1)} %bitcast.52, bf16[2,1536,384]{2,1,0:T(8,128)(2,1)} %collective-permute-done.other_ref), custom_call_target="tpu_custom_call" | custom-call | tf_op jit(solution)/shard_map/phase_2/pallas_call | solution.py:139
  35.7 8.0 %all-to-all-start.1 = ((bf16[16,24,1920]{2,1,0:T(8,128)(2,1)}), bf16[16,24,1920]{2,1,0:T(8,128)(2,1)S(1)}, u32[]{:S(2)}, u32[]{:S(2)}) async-start(bf16[16,24,1920]{2,1,0:T(8,128)(2,1)} %phase_2.1), calls=%async_computation.1 | async-start | bytes 2949120 | tf_op jit(solution)/shard_map/all_to_all | solution.py:351
  43.6 15.2 %phase_0.1 = bf16[16,24,1536]{2,1,0:T(8,128)(2,1)} custom-call(s32[1]{0:T(128)} %bitcast.where_ref, s32[27]{0:T(128)} %reshape.79.mom_ref, bf16[2,1536,384]{2,1,0:T(8,128)(2,1)} %bitcast.53, bf16[2,1536,384]{2,1,0:T(8,128)(2,1)} %collective-permute-done.other_ref), custom_call_target="tpu_custom_call" | custom-call | tf_op jit(solution)/shard_map/phase_0/pallas_call | solution.py:139
  58.8 18.4 %all-to-all-done.1 = bf16[16,24,1920]{2,1,0:T(8,128)(2,1)S(1)} async-done(((bf16[16,24,1920]{2,1,0:T(8,128)(2,1)}), bf16[16,24,1920]{2,1,0:T(8,128)(2,1)S(1)}, u32[]{:S(2)}, u32[]{:S(2)}) %all-to-all-start.1) | async-done | bytes 1474592 | tf_op jit(solution)/shard_map/all_to_all | solution.py:351
  77.2 7.5 %all-to-all-start = ((bf16[16,24,1536]{2,1,0:T(8,128)(2,1)}), bf16[16,24,1536]{2,1,0:T(8,128)(2,1)S(1)}, u32[]{:S(2)}, u32[]{:S(2)}) async-start(bf16[16,24,1536]{2,1,0:T(8,128)(2,1)} %phase_0.1), calls=%async_computation | async-start | bytes 2359296 | tf_op jit(solution)/shard_map/all_to_all | solution.py:351
  85.1 15.6 %all-to-all-done = bf16[16,24,1536]{2,1,0:T(8,128)(2,1)S(1)} async-done(((bf16[16,24,1536]{2,1,0:T(8,128)(2,1)}), bf16[16,24,1536]{2,1,0:T(8,128)(2,1)S(1)}, u32[]{:S(2)}, u32[]{:S(2)}) %all-to-all-start) | async-done | bytes 1179680 | tf_op jit(solution)/shard_map/all_to_all | solution.py:351
  101.2 0.7 copy.41.mom_ref
  101.9 0.7 copy.42.gam_ref
  102.6 9.5 %source.1 = (bf16[24,2,9,16,192]{4,3,2,1,0:T(8,128)(2,1)}, f32[2,256,64]{2,1,0:T(8,128)}, f32[2,4,64,144]{3,2,1,0:T(8,128)}) custom-call(s32[1]{0:T(128)} %bitcast.where_ref, bf16[24,2,16,384]{3,2,1,0:T(8,128)(2,1)} %copy-done.1, bf16[9,2,384,384]{3,2,1,0:T(8,128)(2,1)} %src_ref.1, s32[64,1]{1,0:T(8,128)} %copy.41.mom_ref, s32[64,1]{1,0:T(8,128)} %copy.42.gam_ref, ...), custom_call_target="tpu_custom_call" | custom-call | tf_op jit(solution)/shard_map/source/pallas_call | solution.py:189
  112.8 20.6 %sink.1 = f32[2,64,64]{2,1,0:T(8,128)} custom-call(s32[1]{0:T(128)} %bitcast.where_ref, bf16[24,1536]{1,0:T(8,128)(2,1)} %copy-done.3, bf16[24,1536]{1,0:T(8,128)(2,1)} %copy-done.6, bf16[24,1920]{1,0:T(8,128)(2,1)} %copy-done.2, bf16[24,1920]{1,0:T(8,128)(2,1)} %copy-done.5, bf16[384,6144]{1,0:T(8,128)(2,1)} %all-gather.2.cloned.1.call-done.tau_ref, ...), custom_call_target="tpu_custom_call" | custom-call | tf_op jit(solution)/shard_map/sink/pallas_call | solution.py:297
  133.4 0.9 broadcast_in_dim.20
  134.4 1.9 %broadcast_in_dim.21 = f32[32,1,8192]{2,1,0:T(1,128)} broadcast(f32[8192]{0:T(1024)S(1)} %broadcast_in_dim.20), dimensions={2} | broadcast | bytes 1081344 | tf_op jit(solution)/shard_map/broadcast_in_dim | solution.py:342
  136.3 4.1 %all-to-all-start.2 = ((f32[32,1,8192]{2,1,0:T(1,128)}), f32[32,1,8192]{2,1,0:T(1,128)S(1)}, u32[]{:S(2)}, u32[]{:S(2)}) async-start(f32[32,1,8192]{2,1,0:T(1,128)} %broadcast_in_dim.21), calls=%async_computation.2 | async-start | bytes 2097152 | tf_op jit(solution)/shard_map/all_to_all | solution.py:343
  140.9 16.2 %all-to-all-done.2 = f32[32,1,8192]{2,1,0:T(1,128)S(1)} async-done(((f32[32,1,8192]{2,1,0:T(1,128)}), f32[32,1,8192]{2,1,0:T(1,128)S(1)}, u32[]{:S(2)}, u32[]{:S(2)}) %all-to-all-start.2) | async-done | bytes 1048608 | tf_op jit(solution)/shard_map/all_to_all | solution.py:343
  157.1 0.7 reduce_sum.44
  160.7 0.8 dynamic-update-slice
  161.4 0.7 broadcast_in_dim_reshape.4
  162.1 11.4 %all-reduce = f32[4]{0:T(128)S(1)} all-reduce(f32[4]{0:T(128)S(1)} %dynamic-update-slice), channel_id=1, replica_groups=mesh['ta'=4,'gx'=32] {'ta'}, use_global_device_ids=true, to_apply=%add | all-reduce | flops 4 | bytes 32
  (54 shorter events, 5.5 us)
Async XLA Ops:
  7.2 105.0 %all-gather.2.cloned.1.call-start = ((), (), s32[]{:S(2)}) async-start(), calls=%async_computation.3 | async-start | bytes 5013504 | tf_op jit(solution)/shard_map/all_gather | solution.py:367
  8.3 1.7 collective-permute-start.3
  10.1 3.3 %copy-start.1 = (bf16[24,2,16,384]{3,2,1,0:T(8,128)(2,1)}, bf16[24,2,16,384]{3,2,1,0:T(8,128)(2,1)S(1)}, u32[]{:S(2)}) copy-start(bf16[24,2,16,384]{3,2,1,0:T(8,128)(2,1)S(1)} %maximum_select_fusion.tau_ref) | copy-start | bytes 1769476
  11.4 2.2 %copy-start.7 = (s32[9,3]{0,1:T(4,128)S(1)}, s32[9,3]{0,1:T(4,128)}, u32[]{:S(2)}) copy-start(s32[9,3]{0,1:T(4,128)} %param.12) | copy-start | bytes 328
  13.4 4.8 %copy-start = (bf16[1536,2,384]{2,0,1:T(8,128)(2,1)}, bf16[1536,2,384]{2,0,1:T(8,128)(2,1)S(1)}, u32[]{:S(2)}) copy-start(bf16[1536,2,384]{2,0,1:T(8,128)(2,1)S(1)} %copy.53) | copy-start | bytes 7077892
  13.4 4.7 %collective-permute-start = (bf16[2,1536,384]{2,1,0:T(8,128)(2,1)S(1)}, bf16[2,1536,384]{2,1,0:T(8,128)(2,1)}, u32[]{:S(2)}, u32[]{:S(2)}) collective-permute-start(bf16[2,1536,384]{2,1,0:T(8,128)(2,1)S(1)} %bitcast.51), channel_id=1, source_target_pairs={{0,1},{1,0},{2,3},{3,2},{4,5},{5,4},{6,7},{7,6},{8,9},{9,8},{10,11... | collective-permute-start | bytes 7077896 | tf_op jit(solution)/shard_map/ppermute | solution.py:360
  35.7 41.6 %all-to-all-start.1 = ((bf16[16,24,1920]{2,1,0:T(8,128)(2,1)}), bf16[16,24,1920]{2,1,0:T(8,128)(2,1)S(1)}, u32[]{:S(2)}, u32[]{:S(2)}) async-start(bf16[16,24,1920]{2,1,0:T(8,128)(2,1)} %phase_2.1), calls=%async_computation.1 | async-start | bytes 2949120 | tf_op jit(solution)/shard_map/all_to_all | solution.py:351
  77.2 23.5 %all-to-all-start = ((bf16[16,24,1536]{2,1,0:T(8,128)(2,1)}), bf16[16,24,1536]{2,1,0:T(8,128)(2,1)S(1)}, u32[]{:S(2)}, u32[]{:S(2)}) async-start(bf16[16,24,1536]{2,1,0:T(8,128)(2,1)} %phase_0.1), calls=%async_computation | async-start | bytes 2359296 | tf_op jit(solution)/shard_map/all_to_all | solution.py:351
  84.8 16.4 %copy-start.8 = (s32[64]{0:T(128)S(1)}, s32[64]{0:T(128)}, u32[]{:S(2)}) copy-start(s32[64]{0:T(128)} %param.13) | copy-start | bytes 772
  84.8 17.1 %copy-start.9 = (s32[64]{0:T(128)S(1)}, s32[64]{0:T(128)}, u32[]{:S(2)}) copy-start(s32[64]{0:T(128)} %param.14) | copy-start | bytes 772
  85.0 27.1 %copy-start.2 = (bf16[24,1920]{1,0:T(8,128)(2,1)}, bf16[24,1920]{1,0:T(8,128)(2,1)S(1)}, u32[]{:S(2)}) copy-start(bf16[24,1920]{1,0:T(8,128)(2,1)S(1)} %reduce_sum.43.own2) | copy-start | bytes 276484
  85.0 27.1 %collective-permute-start.2 = (bf16[24,1920]{1,0:T(8,128)(2,1)S(1)}, bf16[24,1920]{1,0:T(8,128)(2,1)S(1)}, u32[]{:S(2)}, u32[]{:S(2)}) collective-permute-start(bf16[24,1920]{1,0:T(8,128)(2,1)S(1)} %reduce_sum.43.own2), channel_id=1, source_target_pairs={{0,1},{1,0},{2,3},{3,2},{4,5},{5,4},{6,7},{7,6},{8,9},{9,8},{10,11... | collective-permute-start | bytes 276488 | tf_op jit(solution)/shard_map/ppermute | solution.py:374
  100.9 11.2 %copy-start.3 = (bf16[24,1536]{1,0:T(8,128)(2,1)}, bf16[24,1536]{1,0:T(8,128)(2,1)S(1)}, u32[]{:S(2)}) copy-start(bf16[24,1536]{1,0:T(8,128)(2,1)S(1)} %reduce_sum.42.own1) | copy-start | bytes 221188
  100.9 11.2 %collective-permute-start.1 = (bf16[24,1536]{1,0:T(8,128)(2,1)S(1)}, bf16[24,1536]{1,0:T(8,128)(2,1)S(1)}, u32[]{:S(2)}, u32[]{:S(2)}) collective-permute-start(bf16[24,1536]{1,0:T(8,128)(2,1)S(1)} %reduce_sum.42.own1), channel_id=1, source_target_pairs={{0,1},{1,0},{2,3},{3,2},{4,5},{5,4},{6,7},{7,6},{8,9},{9,8},{10,11... | collective-permute-start | bytes 221192 | tf_op jit(solution)/shard_map/ppermute | solution.py:373
  112.1 0.6 copy-start.6
  112.2 0.7 copy-start.5
  134.4 6.0 %copy-start.10 = (u32[128]{0:T(128)S(1)}, u32[128]{0:T(128)}, u32[]{:S(2)}) copy-start(u32[128]{0:T(128)} %constant.44) | copy-start | bytes 1540
  136.3 21.7 %copy-start.4 = (f32[2,64,8]{1,2,0:T(8,128)S(1)}, f32[2,64,8]{1,2,0:T(8,128)}, u32[]{:S(2)}) copy-start(f32[2,64,8]{1,2,0:T(8,128)} %param.15) | copy-start | bytes 12292
  136.3 20.9 %all-to-all-start.2 = ((f32[32,1,8192]{2,1,0:T(1,128)}), f32[32,1,8192]{2,1,0:T(1,128)S(1)}, u32[]{:S(2)}, u32[]{:S(2)}) async-start(f32[32,1,8192]{2,1,0:T(1,128)} %broadcast_in_dim.21), calls=%async_computation.2 | async-start | bytes 2097152 | tf_op jit(solution)/shard_map/all_to_all | solution.py:343
Sparse Core Ops, SparseCore 0:
  11.5 72.0 all-gather.1

commit v2 on v1

--- a/solution.py
+++ b/solution.py
@@ -21,6 +21,12 @@
 full_precision = lax.Precision.HIGHEST
 SAME_CORE = [[d for d in range(32) if d % 2 == c] for c in range(2)]
 PAIR = [(d, d ^ 1) for d in range(32)]
+
+
+def shift(x, z):
+    ring = [(i, j, c) for i in range(4) for j in range(4) for c in range(2)]
+    number = lambda i, j, c: i % 4 * 8 + j % 4 * 2 + c
+    return [(number(i, j, c), number(i + x, j + z, c)) for i, j, c in ring]
 
 
 def gamma_tables():
@@ -129,8 +135,20 @@
 
     @pl.when(step == 2 * steps - 1)
     def _():
+        width = acc_ref.shape[1]
+        diagonal = lax.broadcasted_iota(jnp.int32, (384, 384), 0) == lax.broadcasted_iota(
+            jnp.int32, (384, 384), 1
+        )
+        lane = lax.broadcasted_iota(jnp.int32, (384, 128), 1)
+        rest = jnp.zeros((384, 128), F32)
+        for b in range(width // 384):
+            block = acc_ref[:, 384 * b : 384 * b + 384]
+            lost = jnp.where(diagonal, block - block.astype(BF).astype(F32), 0.0)
+            rest = jnp.where(lane == b, jnp.sum(lost, 1, keepdims=True), rest)
         for j in range(16):
-            out_ref[j] = acc_ref[ROWS * j : ROWS * (j + 1), :].astype(BF)
+            at = slice(ROWS * j, ROWS * (j + 1))
+            out_ref[j, :, :width] = acc_ref[at, :].astype(BF)
+            out_ref[j, :, width:] = rest[at].astype(BF)
 
 
 def phase_part(own, other, where, momenta, first, full, half):
@@ -145,11 +163,14 @@
                 pl.BlockSpec((2, CHUNK, 384), lambda c, *_: (0, jnp.minimum(c, steps - 1), 0)),
                 pl.BlockSpec((2, CHUNK, 384), lambda c, *_: (0, jnp.maximum(c - steps, 0), 0)),
             ],
-            out_specs=pl.BlockSpec((16, ROWS, width), lambda c, *_: (0, 0, 0)),
+            out_specs=pl.BlockSpec((16, ROWS, width + 128), lambda c, *_: (0, 0, 0)),
             scratch_shapes=[pltpu.VMEM((384, width), F32)],
         ),
-        out_shape=jax.ShapeDtypeStruct((16, ROWS, width), BF),
+        out_shape=jax.ShapeDtypeStruct((16, ROWS, width + 128), BF),
         compiler_params=pltpu.CompilerParams(vmem_limit_bytes=VMEM),
+        cost_estimate=pl.CostEstimate(
+            flops=4 * 384 * 6144 * width, transcendentals=0, bytes_accessed=6 << 20
+        ),
         name=f"phase_{first}",
     )(where, momenta, own, other)
 
@@ -211,6 +232,9 @@
             jax.ShapeDtypeStruct((2, 4, 64, 144), F32),
         ],
         compiler_params=pltpu.CompilerParams(vmem_limit_bytes=VMEM),
+        cost_estimate=pl.CostEstimate(
+            flops=8 * 384 * 384 * 1728, transcendentals=0, bytes_accessed=8 << 20
+        ),
         name="source",
     )(
         where,
@@ -224,7 +248,7 @@
 
 
 def sink_kernel(
-    where_ref, own1, oth1, own2, oth2, tau_ref, src_ref, left_ref, right_ref, out_ref,
+    where_ref, own1, oth1, own2, oth2, tau_ref, src_ref, left_ref, right_ref, basis_ref, out_ref,
     rows_ref, sink_ref, acc_ref,
 ):
     core = lax.rem(where_ref[0], 2)
@@ -288,12 +312,20 @@
         corr_real -= dot(halves[1], r_imag, 1, 1, full_precision)
         corr_imag += dot(halves[0], r_imag, 1, 1, full_precision)
         corr_imag += dot(halves[1], r_real, 1, 1, full_precision)
-    out_ref[0] = corr_real
-    out_ref[1] = corr_imag
-
-
-def sink_part(where, own1, oth1, own2, oth2, tau, src, left, right):
-    specs = [pl.BlockSpec(memory_space=pltpu.VMEM)] * 8
+    b_real = basis_ref[0]
+    b_imag = basis_ref[1]
+    exact = functools.partial(dot, precision=full_precision)
+    half_real = exact(corr_real, b_real, 1, 0) - exact(corr_imag, b_imag, 1, 0)
+    half_imag = exact(corr_real, b_imag, 1, 0) + exact(corr_imag, b_real, 1, 0)
+    out_ref[:64, :64] = corr_real
+    out_ref[:64, 64:] = corr_imag
+    out_ref[64:, :] = jnp.zeros((8, 128), F32)
+    out_ref[64:, :8] = exact(b_real, half_real, 0, 0) + exact(b_imag, half_imag, 0, 0)
+    out_ref[64:, 8:16] = exact(b_real, half_imag, 0, 0) - exact(b_imag, half_real, 0, 0)
+
+
+def sink_part(where, own1, oth1, own2, oth2, tau, src, left, right, basis):
+    specs = [pl.BlockSpec(memory_space=pltpu.VMEM)] * 9
     return pl.pallas_call(
         sink_kernel,
         grid_spec=pltpu.PrefetchScalarGridSpec(
@@ -307,49 +339,31 @@
                 pltpu.VMEM((512, 288), F32),
             ],
         ),
-        out_shape=jax.ShapeDtypeStruct((2, 64, 64), F32),
+        out_shape=jax.ShapeDtypeStruct((72, 128), F32),
         compiler_params=pltpu.CompilerParams(vmem_limit_bytes=VMEM),
         name="sink",
-    )(where, own1, oth1, own2, oth2, tau, src, left, right)
-
-
-def complex_einsum(form, left_real, left_imag, right_real, right_imag):
-
-    def single(left_part, right_part):
-        return jnp.einsum(
-            form,
-            left_part,
-            right_part,
-            precision=full_precision,
-            preferred_element_type=jnp.float32,
-        )
-
-    return (
-        single(left_real, right_real) - single(left_imag, right_imag),
-        single(left_real, right_imag) + single(left_imag, right_real),
-    )
-
-
-def project(corr_real, corr_imag, ref_vectors):
-    basis_real = ref_vectors[0]
-    basis_imag = ref_vectors[1]
-    half_real, half_imag = complex_einsum("ij,jv->iv", corr_real, corr_imag, basis_real, basis_imag)
-    return complex_einsum("iu,iv->uv", basis_real, -basis_imag, half_real, half_imag)
-
-
-def taken_together(shard, axis):
-    length = lax.axis_size(axis)
-    spread = jnp.broadcast_to(shard[None], (length, *shard.shape))
-    return jnp.sum(lax.all_to_all(spread, axis, 0, 0, tiled=True), axis=0)
-
-
-def picked(shard, axis, root):
-    return lax.dynamic_index_in_dim(lax.all_gather(shard, axis), root, 0, keepdims=False)
-
-
-def scattered(part):
-    got = lax.all_to_all(part, "gx", 0, 0, tiled=True, axis_index_groups=SAME_CORE)
-    return jnp.sum(got.astype(F32), 0).astype(BF)
+    )(where, own1, oth1, own2, oth2, tau, src, left, right, basis)
+
+
+def around(shard, axis):
+    sent = [lax.ppermute(shard, "gx", shift(*(axis * d))) for d in (1, 3, 2)]
+    return shard + sent[0] + sent[1] + sent[2]
+
+
+def exchanged(part):
+    return lax.all_to_all(part, "gx", 0, 0, tiled=True, axis_index_groups=SAME_CORE)
+
+
+def summed(got, chip):
+    total = jnp.sum(got.astype(F32), 0)
+    width = total.shape[1] - 128
+    lane = lax.broadcasted_iota(jnp.int32, (ROWS, width), 1)
+    row = lax.broadcasted_iota(jnp.int32, (ROWS, width), 0)
+    rest = jnp.zeros((ROWS, width), F32)
+    for b in range(width // 384):
+        diagonal = lane == 384 * b + ROWS * chip + row
+        rest = jnp.where(diagonal, total[:, width + b : width + b + 1], rest)
+    return (total[:, :width] + rest).astype(BF)
 
 
 def body(eigvecs, perambulators, source_blocks, momenta, op_momentum, op_gamma, ref_vectors):
@@ -366,21 +380,31 @@
     part = jnp.where(core == 0, tau[..., :192], tau[..., 192:]).reshape(ROWS, 6144)
     tau_all = lax.all_gather(part, "gx", axis=0, tiled=True, axis_index_groups=SAME_CORE)
     flat = momenta.reshape(-1)
-    first = phase_part(own, other, where, flat, 0, 2, 0)
-    own1 = scattered(first)
-    second = phase_part(own, other, where, flat, 2, 2, 1)
-    own2 = scattered(second)
+    first = phase_part(own, other, where, flat, 2, 2, 1)
+    got2 = exchanged(first)
+    second = phase_part(own, other, where, flat, 0, 2, 0)
+    tau, second = lax.optimization_barrier((tau, second))
+    got1 = exchanged(second)
+    src, left, right = source_part(tau, source_blocks, op_momentum, op_gamma, where)
+    got1, got2, src = lax.optimization_barrier((got1, got2, src))
+    own1 = summed(got1, device // 2)
+    own2 = summed(got2, device // 2)
     oth1 = lax.ppermute(own1, "gx", PAIR)
     oth2 = lax.ppermute(own2, "gx", PAIR)
-    src, left, right = source_part(tau, source_blocks, op_momentum, op_gamma, where)
-    corr = sink_part(where, own1, oth1, own2, oth2, tau_all, src, left, right)
-    corr = taken_together(corr.reshape(-1), "gx").reshape(2, 64, 64)
-    proj_real, proj_imag = project(corr[0], corr[1], ref_vectors)
-    raw_pair = jnp.stack([proj_real, proj_imag])
-    local_square = jnp.mean(raw_pair * raw_pair)
-    first_square = picked(local_square, "ta", 0)
-    scale_factor = lax.rsqrt(first_square + 1e-06)
-    return (corr[None], (raw_pair * scale_factor)[None])
+    corr = sink_part(where, own1, oth1, own2, oth2, tau_all, src, left, right, ref_vectors)
+    corr = corr + lax.ppermute(corr, "gx", PAIR)
+    raw = corr[64:]
+    first_raw = jnp.where(lax.axis_index("ta") == 0, raw, 0.0)
+    for t in (1, 3, 2):
+        first_raw = first_raw + lax.ppermute(raw, "ta", [(0, t)])
+    corr = jnp.concatenate([corr, first_raw], 0)
+    corr = around(corr, np.array([1, 0]))
+    corr = around(corr, np.array([0, 1]))
+    first_raw = corr[72:]
+    scale_factor = lax.rsqrt(jnp.sum(first_raw * first_raw) * (1.0 / 128.0) + 1e-06)
+    correlator = jnp.stack([corr[:64, :64], corr[:64, 64:]])[None]
+    raw = jnp.stack([corr[64:72, :8], corr[64:72, 8:16]])
+    return (correlator, (raw * scale_factor)[None])
 
 
 def solution(mesh):

time: 182 us -> 164 us (0.901)
  waiting for transfers between devices: 55.3 us -> 38.3 us
  blocking collectives: 11.4 us -> 0 us
  starting transfers between devices: 20.2 us -> 30.8 us
  other arithmetic: 2.57 us -> 4.52 us
    all_to_all x3 -> x2, waiting for transfers between devices: 50.2 us -> 20.3 us  [exchanged(): lax.all_to_all(part, 'gx', 0, 0, tiled=True, axis_index_groups=SAME_CORE)]
    ppermute x0 -> x10, starting transfers between devices: none -> 14.7 us  [the longest x3 7.66 us: body(): first_raw = first_raw + lax.ppermute(raw, 'ta', [(0, t)])]
    ppermute x0 -> x10, waiting for transfers between devices: none -> 12.3 us  [the longest x6 9.98 us: around(): sent = [lax.ppermute(shard, 'gx', shift(*axis * d)) for d in (1, 3, 2)]]
    unnamed x1 -> x0, blocking collectives: 11.4 us -> none
    all_to_all x3 -> x2, starting transfers between devices: 19.6 us -> 15 us  [exchanged(): lax.all_to_all(part, 'gx', 0, 0, tiled=True, axis_index_groups=SAME_CORE)]
    broadcast_in_dim x2 -> x0, local copies, waits for them, and re-layouts: 2.83 us -> none  [taken_together(): spread = jnp.broadcast_to(shard[None], (length, *shard.shape))]
  transfers between devices with their start and end apart: 8 -> 17, of which waited for: 5 -> 11; matrix products, arithmetic and copies ran while one was open for 3% -> 4% of each run, Pallas kernels for 23% -> 26%
where the time goes in v2:
time: 164 us; the launch traced here: 163 us
  Pallas kernels  64 us (39%)
  waiting for transfers between devices  38.3 us (23%)
  starting transfers between devices  30.8 us (19%)
  between operations  15 us (9%)
  local copies, waits for them, and re-layouts  10.6 us (6%)
  other arithmetic  4.52 us (3%)
    pallas_call x2, Pallas kernels, phase_part(): pl.pallas_call(functools.partial(phase_kernel, first, full, half, steps),...  32.9 us
    pallas_call x1, Pallas kernels, sink_part(): pl.pallas_call(sink_kernel, grid_spec=pltpu.PrefetchScalarGridSpec(num_sc...  21.5 us
    all_to_all x2, waiting for transfers between devices, exchanged(): lax.all_to_all(part, 'gx', 0, 0, tiled=True, axis_index_groups=SAME_CORE)  20.3 us
    all_to_all x2, starting transfers between devices, exchanged(): lax.all_to_all(part, 'gx', 0, 0, tiled=True, axis_index_groups=SAME_CORE)  15 us
    ppermute x6, waiting for transfers between devices, around(): sent = [lax.ppermute(shard, 'gx', shift(*axis * d)) for d in (1, 3, 2)]  9.98 us
    pallas_call x1, Pallas kernels, source_part(): pl.pallas_call(source_kernel, grid_spec=pltpu.PrefetchScalarGridSpec(num_...  9.59 us
    ppermute x3, starting transfers between devices, body(): first_raw = first_raw + lax.ppermute(raw, 'ta', [(0, t)])  7.66 us
    ppermute x6, starting transfers between devices, around(): sent = [lax.ppermute(shard, 'gx', shift(*axis * d)) for d in (1, 3, 2)]  6.7 us
  transfers between devices with their start and end apart: 17, of which 11 were waited for; matrix products, arithmetic and copies ran while one was open for 4% of the time, Pallas kernels for 26%

profile of v2, /device:TPU:0, one launch (start us, length us, event | category | flops | bytes accessed | tf_op | source)
XLA Modules:
  0.0 163.2 jit_solution(8258075958885100918)
XLA Ops:
  8.4 1.5 collective-permute-done
  11.0 2.2 %reshape.50 = bf16[24,6144]{1,0:T(8,128)(2,1)} reshape(bf16[24,2,16,192]{3,2,1,0:T(8,128)(2,1)} %slice_select_fusion) | data formatting | bytes 589824 | tf_op jit(solution)/shard_map/reshape | solution.py:380
  13.3 1.7 %copy.27 = bf16[1536,2,384]{2,0,1:T(8,128)(2,1)} copy(bf16[1536,2,384]{2,1,0:T(2,128)(2,1)S(1)} %bitcast.24) | data formatting | bytes 4718592 | tf_op jit(solution)/shard_map/reshape | solution.py:373
  15.9 3.9 %collective-permute-done.1.other_ref = bf16[2,1536,384]{2,1,0:T(8,128)(2,1)S(1)} collective-permute-done((bf16[2,1536,384]{2,1,0:T(8,128)(2,1)}, bf16[2,1536,384]{2,1,0:T(8,128)(2,1)S(1)}, u32[]{:S(2)}, u32[]{:S(2)}) %collective-permute-start.1) | collective-permute-done | bytes 2359328 | tf_op jit(solution)/shard_map/ppermute | solution.py:374
  19.8 1.5 copy-done.10
  21.3 15.1 %phase_0.1 = bf16[16,24,1664]{2,1,0:T(8,128)(2,1)} custom-call(s32[1]{0:T(128)} %bitcast.where_ref, s32[27]{0:T(128)} %reshape.48.mom_ref, bf16[2,1536,384]{2,1,0:T(8,128)(2,1)} %bitcast.23.own_ref, bf16[2,1536,384]{2,1,0:T(8,128)(2,1)} %copy-done.10), custom_call_target="tpu_custom_call" | custom-call | flops 14495514624 | bytes 6291456 | tf_op jit(solution)/shard_map/phase_0/pallas_call | solution.py:157
  36.3 8.0 %all-to-all-start = ((bf16[16,24,1664]{2,1,0:T(8,128)(2,1)}), bf16[16,24,1664]{2,1,0:T(8,128)(2,1)S(1)}, u32[]{:S(2)}, u32[]{:S(2)}) async-start(bf16[16,24,1664]{2,1,0:T(8,128)(2,1)} %phase_0.1), calls=%async_computation | async-start | bytes 2555904 | tf_op jit(solution)/shard_map/all_to_all | solution.py:354
  44.3 17.8 %phase_2.1 = bf16[16,24,2048]{2,1,0:T(8,128)(2,1)} custom-call(s32[1]{0:T(128)} %bitcast.where_ref, s32[27]{0:T(128)} %reshape.48.mom_ref, bf16[2,1536,384]{2,1,0:T(8,128)(2,1)} %bitcast.23.own_ref, bf16[2,1536,384]{2,1,0:T(8,128)(2,1)} %copy-done.10), custom_call_target="tpu_custom_call" | custom-call | flops 18119393280 | bytes 6291456 | tf_op jit(solution)/shard_map/phase_2/pallas_call | solution.py:157
  62.1 10.7 %all-to-all-done = bf16[16,24,1664]{2,1,0:T(8,128)(2,1)S(1)} async-done(((bf16[16,24,1664]{2,1,0:T(8,128)(2,1)}), bf16[16,24,1664]{2,1,0:T(8,128)(2,1)S(1)}, u32[]{:S(2)}, u32[]{:S(2)}) %all-to-all-start) | async-done | bytes 1277984 | tf_op jit(solution)/shard_map/all_to_all | solution.py:354
  72.9 7.0 %all-to-all-start.1 = ((bf16[16,24,2048]{2,1,0:T(8,128)(2,1)}), bf16[16,24,2048]{2,1,0:T(8,128)(2,1)S(1)}, u32[]{:S(2)}, u32[]{:S(2)}) async-start(bf16[16,24,2048]{2,1,0:T(8,128)(2,1)} %phase_2.1), calls=%async_computation.1 | async-start | bytes 3145728 | tf_op jit(solution)/shard_map/all_to_all | solution.py:354
  81.3 9.6 %source.1 = (bf16[24,2,9,16,192]{4,3,2,1,0:T(8,128)(2,1)}, f32[2,256,64]{2,1,0:T(8,128)}, f32[2,4,64,144]{3,2,1,0:T(8,128)}) custom-call(s32[1]{0:T(128)} %bitcast.where_ref, bf16[24,2,16,384]{3,2,1,0:T(8,128)(2,1)} %copy-done, bf16[9,2,384,384]{3,2,1,0:T(8,128)(2,1)} %src_ref.1, s32[64,1]{1,0:T(8,128)} %copy.20.mom_ref, s32[64,1]{1,0:T(8,128)} %copy.21.gam_ref, ...), custom_call_target="tpu_custom_call" | custom-call | flops 2038431744 | bytes 8388608 | tf_op jit(solution)/shard_map/source/pallas_call | solution.py:210
  90.9 9.6 %all-to-all-done.1 = bf16[16,24,2048]{2,1,0:T(8,128)(2,1)S(1)} async-done(((bf16[16,24,2048]{2,1,0:T(8,128)(2,1)}), bf16[16,24,2048]{2,1,0:T(8,128)(2,1)S(1)}, u32[]{:S(2)}, u32[]{:S(2)}) %all-to-all-start.1) | async-done | bytes 1572896 | tf_op jit(solution)/shard_map/all_to_all | solution.py:354
  104.2 21.5 %sink.1 = f32[72,128]{1,0:T(8,128)} custom-call(s32[1]{0:T(128)} %bitcast.where_ref, bf16[24,1536]{1,0:T(8,128)(2,1)} %copy-done.3, bf16[24,1536]{1,0:T(8,128)(2,1)} %copy-done.5, bf16[24,1920]{1,0:T(8,128)(2,1)} %copy-done.2, bf16[24,1920]{1,0:T(8,128)(2,1)} %copy-done.4, bf16[384,6144]{1,0:T(8,128)(2,1)} %all-gather.2.cloned.1.call-done.tau_ref, ...), custom_call_target="tpu_custom_call" | custom-call | tf_op jit(solution)/shard_map/sink/pallas_call | solution.py:329
  127.9 5.1 %collective-permute-start.7 = (f32[8,128]{1,0:T(8,128)S(1)}, f32[8,128]{1,0:T(8,128)S(1)}, u32[]{:S(2)}, u32[]{:S(2)}) collective-permute-start(f32[8,128]{1,0:T(8,128)S(1)} %slice.89), channel_id=1, source_target_pairs={{0,64},{1,65},{2,66},{3,67},{4,68},{5,69},{6,70},{7,71},{8,72},{9,... | collective-permute-start | bytes 12296 | tf_op jit(solution)/shard_map/ppermute | solution.py:399
  133.0 1.3 collective-permute-start.6
  134.3 1.3 collective-permute-start.5
  135.6 1.3 collective-permute-done.5
  137.6 2.5 %collective-permute-start.9 = (f32[80,128]{1,0:T(8,128)S(1)}, f32[80,128]{1,0:T(8,128)S(1)}, u32[]{:S(2)}, u32[]{:S(2)}) collective-permute-start(f32[80,128]{1,0:T(8,128)S(1)} %pad_maximum_fusion), channel_id=1, source_target_pairs={{0,24},{1,25},{2,26},{3,27},{4,28},{5,29},{6,30},{7,31},{8,0},{9,1... | collective-permute-start | bytes 122888 | tf_op jit(solution)/shard_map/ppermute | solution.py:349
  140.1 2.9 %collective-permute-done.10 = f32[80,128]{1,0:T(8,128)S(1)} collective-permute-done((f32[80,128]{1,0:T(8,128)S(1)}, f32[80,128]{1,0:T(8,128)S(1)}, u32[]{:S(2)}, u32[]{:S(2)}) %collective-permute-start.10) | collective-permute-done | bytes 40992 | tf_op jit(solution)/shard_map/ppermute | solution.py:349
  143.0 2.4 %collective-permute-done.8 = f32[80,128]{1,0:T(8,128)S(1)} collective-permute-done((f32[80,128]{1,0:T(8,128)S(1)}, f32[80,128]{1,0:T(8,128)S(1)}, u32[]{:S(2)}, u32[]{:S(2)}) %collective-permute-start.8) | collective-permute-done | bytes 40992 | tf_op jit(solution)/shard_map/ppermute | solution.py:349
  145.3 1.5 collective-permute-start.13
  146.8 1.6 collective-permute-start.12
  148.9 2.0 %collective-permute-done.13 = f32[80,128]{1,0:T(8,128)S(1)} collective-permute-done((f32[80,128]{1,0:T(8,128)S(1)}, f32[80,128]{1,0:T(8,128)S(1)}, u32[]{:S(2)}, u32[]{:S(2)}) %collective-permute-start.13) | collective-permute-done | bytes 40992 | tf_op jit(solution)/shard_map/ppermute | solution.py:349
  150.9 2.7 %collective-permute-done.11 = f32[80,128]{1,0:T(8,128)S(1)} collective-permute-done((f32[80,128]{1,0:T(8,128)S(1)}, f32[80,128]{1,0:T(8,128)S(1)}, u32[]{:S(2)}, u32[]{:S(2)}) %collective-permute-start.11) | collective-permute-done | bytes 40992 | tf_op jit(solution)/shard_map/ppermute | solution.py:349
  (68 shorter events, 13.6 us)
Async XLA Ops:
  7.2 96.4 %all-gather.2.cloned.1.call-start = ((), (), s32[]{:S(2)}) async-start(), calls=%async_computation.2 | async-start | bytes 5013504 | tf_op jit(solution)/shard_map/all_gather | solution.py:381
  8.3 1.7 %collective-permute-start = (bf16[12,2,16,384]{3,2,1,0:T(8,128)(2,1)S(1)}, bf16[12,2,16,384]{3,2,1,0:T(8,128)(2,1)S(1)}, u32[]{:S(2)}, u32[]{:S(2)}) collective-permute-start(bf16[12,2,16,384]{3,2,1,0:T(8,128)(2,1)S(1)} %copy.23), channel_id=1, source_target_pairs={{0,1},{1,0},{2,3},{3,2},{4,5},{5,4},{6,7},{7,6},{8,9},{9,8},{10,11... | collective-permute-start | bytes 884744 | tf_op jit(solution)/shard_map/ppermute | solution.py:376
  8.4 4.9 %copy-start.1 = (bf16[1,512,3,2,384]{4,3,2,1,0:T(2,128)(2,1)S(1)}, bf16[1,512,3,2,384]{4,3,2,1,0:T(2,128)(2,1)}, u32[]{:S(2)}) copy-start(bf16[1,512,3,2,384]{4,3,2,1,0:T(2,128)(2,1)} %param.9) | copy-start | bytes 7077892
  10.1 5.0 %copy-start = (bf16[24,2,16,384]{3,2,1,0:T(8,128)(2,1)}, bf16[24,2,16,384]{3,2,1,0:T(8,128)(2,1)S(1)}, u32[]{:S(2)}) copy-start(bf16[24,2,16,384]{3,2,1,0:T(8,128)(2,1)S(1)} %maximum_select_fusion.tau_ref) | copy-start | bytes 1769476
  13.3 1.9 %copy-start.7 = (s32[9,3]{0,1:T(4,128)S(1)}, s32[9,3]{0,1:T(4,128)}, u32[]{:S(2)}) copy-start(s32[9,3]{0,1:T(4,128)} %param.12) | copy-start | bytes 328
  15.0 4.7 %collective-permute-start.1 = (bf16[2,1536,384]{2,1,0:T(8,128)(2,1)}, bf16[2,1536,384]{2,1,0:T(8,128)(2,1)S(1)}, u32[]{:S(2)}, u32[]{:S(2)}) collective-permute-start(bf16[2,1536,384]{2,1,0:T(8,128)(2,1)} %bitcast.23.own_ref), channel_id=1, source_target_pairs={{0,1},{1,0},{2,3},{3,2},{4,5},{5,4},{6,7},{7,6},{8,9},{9,8},{10,11... | collective-permute-start | bytes 7077896 | tf_op jit(solution)/shard_map/ppermute | solution.py:374
  36.3 36.5 %all-to-all-start = ((bf16[16,24,1664]{2,1,0:T(8,128)(2,1)}), bf16[16,24,1664]{2,1,0:T(8,128)(2,1)S(1)}, u32[]{:S(2)}, u32[]{:S(2)}) async-start(bf16[16,24,1664]{2,1,0:T(8,128)(2,1)} %phase_0.1), calls=%async_computation | async-start | bytes 2555904 | tf_op jit(solution)/shard_map/all_to_all | solution.py:354
  62.1 17.7 %copy-start.8 = (s32[64]{0:T(128)S(1)}, s32[64]{0:T(128)}, u32[]{:S(2)}) copy-start(s32[64]{0:T(128)} %param.13) | copy-start | bytes 772
  62.1 18.5 %copy-start.9 = (s32[64]{0:T(128)S(1)}, s32[64]{0:T(128)}, u32[]{:S(2)}) copy-start(s32[64]{0:T(128)} %param.14) | copy-start | bytes 772
  72.9 27.7 %all-to-all-start.1 = ((bf16[16,24,2048]{2,1,0:T(8,128)(2,1)}), bf16[16,24,2048]{2,1,0:T(8,128)(2,1)S(1)}, u32[]{:S(2)}, u32[]{:S(2)}) async-start(bf16[16,24,2048]{2,1,0:T(8,128)(2,1)} %phase_2.1), calls=%async_computation.1 | async-start | bytes 3145728 | tf_op jit(solution)/shard_map/all_to_all | solution.py:354
  100.5 2.2 %copy-start.6 = (f32[2,64,8]{1,2,0:T(8,128)S(1)}, f32[2,64,8]{1,2,0:T(8,128)}, u32[]{:S(2)}) copy-start(f32[2,64,8]{1,2,0:T(8,128)} %param.15) | copy-start | bytes 12292
  101.2 2.4 %copy-start.2 = (bf16[24,1920]{1,0:T(8,128)(2,1)}, bf16[24,1920]{1,0:T(8,128)(2,1)S(1)}, u32[]{:S(2)}) copy-start(bf16[24,1920]{1,0:T(8,128)(2,1)S(1)} %fusion.own2) | copy-start | bytes 276484
  101.2 2.3 %collective-permute-start.3 = (bf16[24,1920]{1,0:T(8,128)(2,1)S(1)}, bf16[24,1920]{1,0:T(8,128)(2,1)S(1)}, u32[]{:S(2)}, u32[]{:S(2)}) collective-permute-start(bf16[24,1920]{1,0:T(8,128)(2,1)S(1)} %fusion.own2), channel_id=1, source_target_pairs={{0,1},{1,0},{2,3},{3,2},{4,5},{5,4},{6,7},{7,6},{8,9},{9,8},{10,11... | collective-permute-start | bytes 276488 | tf_op jit(solution)/shard_map/ppermute | solution.py:393
  101.9 1.7 %collective-permute-start.2 = (bf16[24,1536]{1,0:T(8,128)(2,1)S(1)}, bf16[24,1536]{1,0:T(8,128)(2,1)S(1)}, u32[]{:S(2)}, u32[]{:S(2)}) collective-permute-start(bf16[24,1536]{1,0:T(8,128)(2,1)S(1)} %fusion.1.own1), channel_id=1, source_target_pairs={{0,1},{1,0},{2,3},{3,2},{4,5},{5,4},{6,7},{7,6},{8,9},{9,8},{10,11... | collective-permute-start | bytes 221192 | tf_op jit(solution)/shard_map/ppermute | solution.py:392
  125.7 1.4 collective-permute-start.4
  127.9 7.7 %collective-permute-start.7 = (f32[8,128]{1,0:T(8,128)S(1)}, f32[8,128]{1,0:T(8,128)S(1)}, u32[]{:S(2)}, u32[]{:S(2)}) collective-permute-start(f32[8,128]{1,0:T(8,128)S(1)} %slice.89), channel_id=1, source_target_pairs={{0,64},{1,65},{2,66},{3,67},{4,68},{5,69},{6,70},{7,71},{8,72},{9,... | collective-permute-start | bytes 12296 | tf_op jit(solution)/shard_map/ppermute | solution.py:399
  133.0 2.6 %collective-permute-start.6 = (f32[8,128]{1,0:T(8,128)S(1)}, f32[8,128]{1,0:T(8,128)S(1)}, u32[]{:S(2)}, u32[]{:S(2)}) collective-permute-start(f32[8,128]{1,0:T(8,128)S(1)} %slice.89), channel_id=1, source_target_pairs={{0,96},{1,97},{2,98},{3,99},{4,100},{5,101},{6,102},{7,103},{8,104... | collective-permute-start | bytes 12296 | tf_op jit(solution)/shard_map/ppermute | solution.py:399
  134.3 2.6 %collective-permute-start.5 = (f32[8,128]{1,0:T(8,128)S(1)}, f32[8,128]{1,0:T(8,128)S(1)}, u32[]{:S(2)}, u32[]{:S(2)}) collective-permute-start(f32[8,128]{1,0:T(8,128)S(1)} %slice.89), channel_id=1, source_target_pairs={{0,32},{1,33},{2,34},{3,35},{4,36},{5,37},{6,38},{7,39},{8,40},{9,... | collective-permute-start | bytes 12296 | tf_op jit(solution)/shard_map/ppermute | solution.py:399
  136.9 6.0 %collective-permute-start.10 = (f32[80,128]{1,0:T(8,128)S(1)}, f32[80,128]{1,0:T(8,128)S(1)}, u32[]{:S(2)}, u32[]{:S(2)}) collective-permute-start(f32[80,128]{1,0:T(8,128)S(1)} %pad_maximum_fusion), channel_id=1, source_target_pairs={{0,16},{1,17},{2,18},{3,19},{4,20},{5,21},{6,22},{7,23},{8,24},{9,... | collective-permute-start | bytes 122888 | tf_op jit(solution)/shard_map/ppermute | solution.py:349
  137.6 5.3 %collective-permute-start.9 = (f32[80,128]{1,0:T(8,128)S(1)}, f32[80,128]{1,0:T(8,128)S(1)}, u32[]{:S(2)}, u32[]{:S(2)}) collective-permute-start(f32[80,128]{1,0:T(8,128)S(1)} %pad_maximum_fusion), channel_id=1, source_target_pairs={{0,24},{1,25},{2,26},{3,27},{4,28},{5,29},{6,30},{7,31},{8,0},{9,1... | collective-permute-start | bytes 122888 | tf_op jit(solution)/shard_map/ppermute | solution.py:349
  140.1 5.2 %collective-permute-start.8 = (f32[80,128]{1,0:T(8,128)S(1)}, f32[80,128]{1,0:T(8,128)S(1)}, u32[]{:S(2)}, u32[]{:S(2)}) collective-permute-start(f32[80,128]{1,0:T(8,128)S(1)} %pad_maximum_fusion), channel_id=1, source_target_pairs={{0,8},{1,9},{2,10},{3,11},{4,12},{5,13},{6,14},{7,15},{8,16},{9,17... | collective-permute-start | bytes 122888 | tf_op jit(solution)/shard_map/ppermute | solution.py:349
  145.3 5.6 %collective-permute-start.13 = (f32[80,128]{1,0:T(8,128)S(1)}, f32[80,128]{1,0:T(8,128)S(1)}, u32[]{:S(2)}, u32[]{:S(2)}) collective-permute-start(f32[80,128]{1,0:T(8,128)S(1)} %add_add_fusion.1), channel_id=1, source_target_pairs={{0,4},{1,5},{2,6},{3,7},{4,0},{5,1},{6,2},{7,3},{8,12},{9,13},{10,... | collective-permute-start | bytes 122888 | tf_op jit(solution)/shard_map/ppermute | solution.py:349
  146.8 4.1 %collective-permute-start.12 = (f32[80,128]{1,0:T(8,128)S(1)}, f32[80,128]{1,0:T(8,128)S(1)}, u32[]{:S(2)}, u32[]{:S(2)}) collective-permute-start(f32[80,128]{1,0:T(8,128)S(1)} %add_add_fusion.1), channel_id=1, source_target_pairs={{0,6},{1,7},{2,0},{3,1},{4,2},{5,3},{6,4},{7,5},{8,14},{9,15},{10,... | collective-permute-start | bytes 122888 | tf_op jit(solution)/shard_map/ppermute | solution.py:349
  148.4 5.2 %collective-permute-start.11 = (f32[80,128]{1,0:T(8,128)S(1)}, f32[80,128]{1,0:T(8,128)S(1)}, u32[]{:S(2)}, u32[]{:S(2)}) collective-permute-start(f32[80,128]{1,0:T(8,128)S(1)} %add_add_fusion.1), channel_id=1, source_target_pairs={{0,2},{1,3},{2,4},{3,5},{4,6},{5,7},{6,0},{7,1},{8,10},{9,11},{10,... | collective-permute-start | bytes 122888 | tf_op jit(solution)/shard_map/ppermute | solution.py:349
  (4 other events, 4.5 us)
Sparse Core Ops, SparseCore 0:
  13.4 68.2 all-gather.1

commit v3 on v2

--- a/solution.py
+++ b/solution.py
@@ -176,7 +176,8 @@
 
 
 def source_kernel(
-    where_ref, tau_ref, src_ref, mom_ref, gam_ref, ltab_ref, rtab_ref, out_ref, left_ref, right_ref
+    where_ref, tau_ref, src_ref, mom_ref, gam_ref, ltab_ref, rtab_ref, vec_ref,
+    out_ref, left_ref, right_ref, basis_ref,
 ):
     n = pl.program_id(0)
     x = jnp.concatenate([tau_ref[:, 0].reshape(384, 384), tau_ref[:, 1].reshape(384, 384)], 1)
@@ -189,6 +190,7 @@
 
     @pl.when(n == 0)
     def _():
+        basis_ref[...] = vec_ref[...]
         chosen = (gam_ref[...] == lax.broadcasted_iota(jnp.int32, (64, 16), 1)).astype(BF)
         lane = lax.rem(lax.broadcasted_iota(jnp.int32, (64, 64), 1), MPAD)
         moment = mom_ref[...] == lane
@@ -204,7 +206,7 @@
                 right_ref[q, y] = jnp.where(moment, dot(chosen, rtab_ref[q, y], 1, 0), 0.0)
 
 
-def source_part(tau, source_blocks, op_momentum, op_gamma, where):
+def source_part(tau, source_blocks, op_momentum, op_gamma, ref_vectors, where):
     ltab, rtab = spin_tables()
     whole = lambda shape: pl.BlockSpec(shape, lambda n, *_: (0,) * len(shape))
     return pl.pallas_call(
@@ -219,17 +221,20 @@
                 whole((64, 1)),
                 whole((2, 4, 16, 64)),
                 whole((2, 4, 16, 144)),
+                whole((2, 64, 8)),
             ],
             out_specs=[
                 pl.BlockSpec((ROWS, 2, 1, 16, 192), lambda n, *_: (0, 0, n, 0, 0)),
                 whole((2, 256, 64)),
                 whole((2, 4, 64, 144)),
+                whole((2, 64, 8)),
             ],
         ),
         out_shape=[
             jax.ShapeDtypeStruct((ROWS, 2, NMOM, 16, 192), BF),
             jax.ShapeDtypeStruct((2, 256, 64), F32),
             jax.ShapeDtypeStruct((2, 4, 64, 144), F32),
+            jax.ShapeDtypeStruct((2, 64, 8), F32),
         ],
         compiler_params=pltpu.CompilerParams(vmem_limit_bytes=VMEM),
         cost_estimate=pl.CostEstimate(
@@ -244,14 +249,31 @@
         op_gamma[:, None],
         jnp.asarray(ltab, BF),
         jnp.asarray(rtab, BF),
-    )
+        ref_vectors,
+    )
+
+
+def thirds(value):
+    high = value.astype(BF)
+    rest = value - high.astype(F32)
+    middle = rest.astype(BF)
+    return [high, middle, (rest - middle.astype(F32)).astype(BF)]
 
 
 def sink_kernel(
-    where_ref, own1, oth1, own2, oth2, tau_ref, src_ref, left_ref, right_ref, basis_ref, out_ref,
-    rows_ref, sink_ref, acc_ref,
+    where_ref, own1, oth1, own2, oth2, tau_hbm, src_hbm, left_ref, right_ref, basis_ref, out_ref,
+    rows_ref, sink_ref, acc_ref, tau_ref, src_ref, sem,
 ):
     core = lax.rem(where_ref[0], 2)
+    fetches = []
+    for g in range(4):
+        for q in range(2):
+            source = tau_hbm.at[:, pl.ds(3072 * q + 768 * g, 768)]
+            target = tau_ref.at[q, :, pl.ds(768 * g, 768)]
+            fetches.append(pltpu.make_async_copy(source, target, sem.at[2 * g + q]))
+    fetches.append(pltpu.make_async_copy(src_hbm, src_ref, sem.at[8]))
+    for fetch in fetches:
+        fetch.start()
     rows_ref[...] = jnp.zeros_like(rows_ref)
     for c in range(2):
         one = jnp.where(core == c, own1[...], oth1[...]).astype(F32)
@@ -268,37 +290,41 @@
         [jnp.concatenate([real, -imag], 1), jnp.concatenate([imag, real], 1)], 0
     )
     for g in range(4):
+        fetches[2 * g].wait()
+        fetches[2 * g + 1].wait()
         at = slice(768 * g, 768 * g + 768)
-        here = jnp.concatenate([tau_ref[:, at], tau_ref[:, 3072 + 768 * g : 3840 + 768 * g]], 0)
+        here = jnp.concatenate([tau_ref[0, :, at], tau_ref[1, :, at]], 0)
         got = dot(stacked, here, 1, 0).astype(BF)
         for y in range(4):
             for q in range(2):
                 sink_ref[q, 4 * y + g] = got[384 * q : 384 * q + 384, 192 * y : 192 * y + 192]
     acc_ref[...] = jnp.zeros_like(acc_ref)
+    fetches[8].wait()
 
     def one_row(r, carry):
         at = pl.ds(pl.multiple_of(r * MPAD, MPAD), MPAD)
         left = jnp.concatenate([sink_ref[q, :, at, :].reshape(256, 192) for q in range(2)], 0)
         right = src_ref[r].reshape(288, 192)
-        acc_ref[...] += dot(left, right, 1, 1)
+        acc_ref[...] += dot(right, left, 1, 1)
         return carry
 
-    lax.fori_loop(0, ROWS, one_row, 0)
+    lax.fori_loop(0, ROWS, one_row, 0, unroll=8)
     acc = acc_ref[...]
-    block_real = acc[:256, :144] - acc[256:, 144:]
-    block_imag = acc[:256, 144:] + acc[256:, :144]
+    block_real = acc[:144, :256] - acc[144:, 256:]
+    block_imag = acc[144:, :256] + acc[:144, 256:]
     l_real = left_ref[0]
     l_imag = left_ref[1]
     lifted = jnp.concatenate(
         [jnp.concatenate([l_real, -l_imag], 1), jnp.concatenate([l_imag, l_real], 1)], 0
-    )
+    ).astype(BF)
+    lifted = jnp.concatenate([lifted] * 3, 1)
     spin = lax.rem(lax.broadcasted_iota(jnp.int32, (64, 144), 1), 16) // 4
     corr_real = jnp.zeros((64, 64), F32)
     corr_imag = jnp.zeros((64, 64), F32)
     for y in range(4):
         at = slice(64 * y, 64 * y + 64)
-        both = jnp.concatenate([block_real[at], block_imag[at]], 0)
-        got = dot(lifted, both, 1, 0, full_precision)
+        both = thirds(jnp.concatenate([block_real[:, at], block_imag[:, at]], 1))
+        got = dot(lifted, jnp.concatenate(both, 1), 1, 1)
         halves = []
         for q in range(2):
             total = jnp.zeros((64, 144), F32)
@@ -308,10 +334,12 @@
             halves.append(total)
         r_real = right_ref[0, y]
         r_imag = right_ref[1, y]
-        corr_real += dot(halves[0], r_real, 1, 1, full_precision)
-        corr_real -= dot(halves[1], r_imag, 1, 1, full_precision)
-        corr_imag += dot(halves[0], r_imag, 1, 1, full_precision)
-        corr_imag += dot(halves[1], r_real, 1, 1, full_precision)
+        weights = jnp.concatenate([r_real, r_imag], 0).astype(BF)
+        lhs = jnp.concatenate(thirds(jnp.concatenate(halves, 0)), 0)
+        got = dot(lhs, weights, 1, 1)
+        got = got[:128] + got[128:256] + got[256:]
+        corr_real += got[:64, :64] - got[64:, 64:]
+        corr_imag += got[:64, 64:] + got[64:, :64]
     b_real = basis_ref[0]
     b_imag = basis_ref[1]
     exact = functools.partial(dot, precision=full_precision)
@@ -325,7 +353,9 @@
 
 
 def sink_part(where, own1, oth1, own2, oth2, tau, src, left, right, basis):
-    specs = [pl.BlockSpec(memory_space=pltpu.VMEM)] * 9
+    inside = pl.BlockSpec(memory_space=pltpu.VMEM)
+    outside = pl.BlockSpec(memory_space=pl.ANY)
+    specs = [inside] * 4 + [outside] * 2 + [inside] * 3
     return pl.pallas_call(
         sink_kernel,
         grid_spec=pltpu.PrefetchScalarGridSpec(
@@ -336,7 +366,10 @@
             scratch_shapes=[
                 pltpu.VMEM((2, ROWS, MPAD, 384), F32),
                 pltpu.VMEM((2, 16, 384, 192), BF),
-                pltpu.VMEM((512, 288), F32),
+                pltpu.VMEM((288, 512), F32),
+                pltpu.VMEM((2, 384, 3072), BF),
+                pltpu.VMEM((ROWS, 2, NMOM, 16, 192), BF),
+                pltpu.SemaphoreType.DMA((9,)),
             ],
         ),
         out_shape=jax.ShapeDtypeStruct((72, 128), F32),
@@ -371,6 +404,7 @@
     core = device % 2
     where = device[None]
     own = jnp.transpose(eigvecs.reshape(-1, 2, 384), (1, 0, 2))
+    own, perambulators = lax.optimization_barrier((own, perambulators))
     other = lax.ppermute(own, "gx", PAIR)
     mine = jnp.transpose(perambulators[0], (1, 0, 2, 3, 4)).reshape(12, 2, 16, 384)
     theirs = lax.ppermute(mine, "gx", PAIR)
@@ -385,13 +419,15 @@
     second = phase_part(own, other, where, flat, 0, 2, 0)
     tau, second = lax.optimization_barrier((tau, second))
     got1 = exchanged(second)
-    src, left, right = source_part(tau, source_blocks, op_momentum, op_gamma, where)
+    src, left, right, basis = source_part(
+        tau, source_blocks, op_momentum, op_gamma, ref_vectors, where
+    )
     got1, got2, src = lax.optimization_barrier((got1, got2, src))
     own1 = summed(got1, device // 2)
     own2 = summed(got2, device // 2)
     oth1 = lax.ppermute(own1, "gx", PAIR)
     oth2 = lax.ppermute(own2, "gx", PAIR)
-    corr = sink_part(where, own1, oth1, own2, oth2, tau_all, src, left, right, ref_vectors)
+    corr = sink_part(where, own1, oth1, own2, oth2, tau_all, src, left, right, basis)
     corr = corr + lax.ppermute(corr, "gx", PAIR)
     raw = corr[64:]
     first_raw = jnp.where(lax.axis_index("ta") == 0, raw, 0.0)

time: 164 us -> 155 us (0.945)
  Pallas kernels: 64 us -> 56.6 us
  local copies, waits for them, and re-layouts: 10.6 us -> 8.43 us
    pallas_call x1, Pallas kernels: 21.5 us -> 14 us  [sink_part(): pl.pallas_call(sink_kernel, grid_spec=pltpu.PrefetchScalarGridSpec(num_sc...]
  transfers between devices with their start and end apart: 17 -> 17, of which waited for: 11 -> 12; matrix products, arithmetic and copies ran while one was open for 4% -> 3% of each run, Pallas kernels for 26% -> 28%
where the time goes in v3:
time: 155 us; the launch traced here: 154 us
  Pallas kernels  56.6 us (37%)
  waiting for transfers between devices  37.5 us (24%)
  starting transfers between devices  31.7 us (20%)
  between operations  15 us (10%)
  local copies, waits for them, and re-layouts  8.43 us (5%)
  other arithmetic  4.52 us (3%)
    pallas_call x2, Pallas kernels, phase_part(): pl.pallas_call(functools.partial(phase_kernel, first, full, half, steps),...  32.9 us
    all_to_all x2, waiting for transfers between devices, exchanged(): lax.all_to_all(part, 'gx', 0, 0, tiled=True, axis_index_groups=SAME_CORE)  20.1 us
    all_to_all x2, starting transfers between devices, exchanged(): lax.all_to_all(part, 'gx', 0, 0, tiled=True, axis_index_groups=SAME_CORE)  15 us
    pallas_call x1, Pallas kernels, sink_part(): pl.pallas_call(sink_kernel, grid_spec=pltpu.PrefetchScalarGridSpec(num_sc...  14 us
    pallas_call x1, Pallas kernels, source_part(): pl.pallas_call(source_kernel, grid_spec=pltpu.PrefetchScalarGridSpec(num_...  9.64 us
    ppermute x6, waiting for transfers between devices, around(): sent = [lax.ppermute(shard, 'gx', shift(*axis * d)) for d in (1, 3, 2)]  8.69 us
    ppermute x3, starting transfers between devices, body(): first_raw = first_raw + lax.ppermute(raw, 'ta', [(0, t)])  7.69 us
    ppermute x6, starting transfers between devices, around(): sent = [lax.ppermute(shard, 'gx', shift(*axis * d)) for d in (1, 3, 2)]  7.49 us
  transfers between devices with their start and end apart: 17, of which 12 were waited for; matrix products, arithmetic and copies ran while one was open for 3% of the time, Pallas kernels for 28%

profile of v3, /device:TPU:0, one launch (start us, length us, event | category | flops | bytes accessed | tf_op | source)
XLA Modules:
  0.0 153.7 jit_solution(14301649025970725224)
XLA Ops:
  7.2 2.0 %copy.27 = bf16[1536,2,384]{2,0,1:T(8,128)(2,1)S(1)} copy(bf16[1536,2,384]{2,1,0:T(2,128)(2,1)} %bitcast.24) | data formatting | bytes 4718592 | tf_op jit(solution)/shard_map/reshape | solution.py:406
  9.5 1.5 %collective-permute-done = bf16[12,2,16,384]{3,2,1,0:T(8,128)(2,1)S(1)} collective-permute-done((bf16[12,2,16,384]{3,2,1,0:T(8,128)(2,1)S(1)}, bf16[12,2,16,384]{3,2,1,0:T(8,128)(2,1)S(1)}, u32[]{:S(2)}, u32[]{:S(2)}) %collective-permute-start) | collective-permute-done | bytes 294944 | tf_op jit(solution)/shard_map/ppermute | solution.py:410
  12.1 2.2 %reshape.50 = bf16[24,6144]{1,0:T(8,128)(2,1)} reshape(bf16[24,2,16,192]{3,2,1,0:T(8,128)(2,1)} %slice_select_fusion) | data formatting | bytes 589824 | tf_op jit(solution)/shard_map/reshape | solution.py:414
  15.3 3.8 %collective-permute-done.1.other_ref = bf16[2,1536,384]{2,1,0:T(8,128)(2,1)} collective-permute-done((bf16[2,1536,384]{2,1,0:T(8,128)(2,1)S(1)}, bf16[2,1536,384]{2,1,0:T(8,128)(2,1)}, u32[]{:S(2)}, u32[]{:S(2)}) %collective-permute-start.1) | collective-permute-done | bytes 2359328 | tf_op jit(solution)/shard_map/ppermute | solution.py:408
  19.1 15.1 %phase_0.1 = bf16[16,24,1664]{2,1,0:T(8,128)(2,1)} custom-call(s32[1]{0:T(128)} %bitcast.where_ref, s32[27]{0:T(128)} %reshape.49.mom_ref, bf16[2,1536,384]{2,1,0:T(8,128)(2,1)} %bitcast.26, bf16[2,1536,384]{2,1,0:T(8,128)(2,1)} %collective-permute-done.1.other_ref), custom_call_target="tpu_custom_call" | custom-call | flops 14495514624 | bytes 6291456 | tf_op jit(solution)/shard_map/phase_0/pallas_call | solution.py:157
  34.2 7.9 %all-to-all-start = ((bf16[16,24,1664]{2,1,0:T(8,128)(2,1)}), bf16[16,24,1664]{2,1,0:T(8,128)(2,1)S(1)}, u32[]{:S(2)}, u32[]{:S(2)}) async-start(bf16[16,24,1664]{2,1,0:T(8,128)(2,1)} %phase_0.1), calls=%async_computation | async-start | bytes 2555904 | tf_op jit(solution)/shard_map/all_to_all | solution.py:387
  42.1 17.8 %phase_2.1 = bf16[16,24,2048]{2,1,0:T(8,128)(2,1)} custom-call(s32[1]{0:T(128)} %bitcast.where_ref, s32[27]{0:T(128)} %reshape.49.mom_ref, bf16[2,1536,384]{2,1,0:T(8,128)(2,1)} %bitcast.27, bf16[2,1536,384]{2,1,0:T(8,128)(2,1)} %collective-permute-done.1.other_ref), custom_call_target="tpu_custom_call" | custom-call | flops 18119393280 | bytes 6291456 | tf_op jit(solution)/shard_map/phase_2/pallas_call | solution.py:157
  60.0 7.5 %all-to-all-done = bf16[16,24,1664]{2,1,0:T(8,128)(2,1)S(1)} async-done(((bf16[16,24,1664]{2,1,0:T(8,128)(2,1)}), bf16[16,24,1664]{2,1,0:T(8,128)(2,1)S(1)}, u32[]{:S(2)}, u32[]{:S(2)}) %all-to-all-start) | async-done | bytes 1277984 | tf_op jit(solution)/shard_map/all_to_all | solution.py:387
  67.5 7.0 %all-to-all-start.1 = ((bf16[16,24,2048]{2,1,0:T(8,128)(2,1)}), bf16[16,24,2048]{2,1,0:T(8,128)(2,1)S(1)}, u32[]{:S(2)}, u32[]{:S(2)}) async-start(bf16[16,24,2048]{2,1,0:T(8,128)(2,1)} %phase_2.1), calls=%async_computation.1 | async-start | bytes 3145728 | tf_op jit(solution)/shard_map/all_to_all | solution.py:387
  76.6 9.6 %source.1 = (bf16[24,2,9,16,192]{4,3,2,1,0:T(8,128)(2,1)}, f32[2,256,64]{2,1,0:T(8,128)}, f32[2,4,64,144]{3,2,1,0:T(8,128)}, f32[2,64,8]{2,1,0:T(8,128)}) custom-call(s32[1]{0:T(128)} %bitcast.where_ref, bf16[24,2,16,384]{3,2,1,0:T(8,128)(2,1)} %copy-done, bf16[9,2,384,384]{3,2,1,0:T(8,128)(2,1)} %src_ref.1, s32[64,1]{1,0:T(8,128)} %copy.20.mom_ref, ...), custom_call_target="tpu_custom_call" | custom-call | flops 2038431744 | bytes 8388608 | tf_op jit(solution)/shard_map/source/pallas_call | solution.py:212
  86.3 12.6 %all-to-all-done.1 = bf16[16,24,2048]{2,1,0:T(8,128)(2,1)S(1)} async-done(((bf16[16,24,2048]{2,1,0:T(8,128)(2,1)}), bf16[16,24,2048]{2,1,0:T(8,128)(2,1)S(1)}, u32[]{:S(2)}, u32[]{:S(2)}) %all-to-all-start.1) | async-done | bytes 1572896 | tf_op jit(solution)/shard_map/all_to_all | solution.py:387
  102.6 14.0 %sink.1 = f32[72,128]{1,0:T(8,128)} custom-call(s32[1]{0:T(128)} %bitcast.where_ref, bf16[24,1536]{1,0:T(8,128)(2,1)} %copy-done.4, bf16[24,1536]{1,0:T(8,128)(2,1)} %copy-done.6, bf16[24,1920]{1,0:T(8,128)(2,1)} %copy-done.2, bf16[24,1920]{1,0:T(8,128)(2,1)} %copy-done.5, bf16[384,6144]{1,0:T(8,128)(2,1)} %all-gather.2.cloned.1.call-done.tau_hbm, ...), custom_call_target="tpu_custom_call" | custom-call | tf_op jit(solution)/shard_map/sink/pallas_call | solution.py:359
  118.9 5.1 %collective-permute-start.7 = (f32[8,128]{1,0:T(8,128)S(1)}, f32[8,128]{1,0:T(8,128)S(1)}, u32[]{:S(2)}, u32[]{:S(2)}) collective-permute-start(f32[8,128]{1,0:T(8,128)S(1)} %slice.89), channel_id=1, source_target_pairs={{0,64},{1,65},{2,66},{3,67},{4,68},{5,69},{6,70},{7,71},{8,72},{9,... | collective-permute-start | bytes 12296 | tf_op jit(solution)/shard_map/ppermute | solution.py:435
  124.1 1.3 collective-permute-start.6
  125.4 1.3 collective-permute-start.5
  126.7 1.3 collective-permute-done.5
  128.0 1.7 %collective-permute-start.10 = (f32[80,128]{1,0:T(8,128)S(1)}, f32[80,128]{1,0:T(8,128)S(1)}, u32[]{:S(2)}, u32[]{:S(2)}) collective-permute-start(f32[80,128]{1,0:T(8,128)S(1)} %pad_maximum_fusion), channel_id=1, source_target_pairs={{0,16},{1,17},{2,18},{3,19},{4,20},{5,21},{6,22},{7,23},{8,24},{9,... | collective-permute-start | bytes 122888 | tf_op jit(solution)/shard_map/ppermute | solution.py:382
  130.4 1.3 collective-permute-start.8
  131.7 2.3 %collective-permute-done.10 = f32[80,128]{1,0:T(8,128)S(1)} collective-permute-done((f32[80,128]{1,0:T(8,128)S(1)}, f32[80,128]{1,0:T(8,128)S(1)}, u32[]{:S(2)}, u32[]{:S(2)}) %collective-permute-start.10) | collective-permute-done | bytes 40992 | tf_op jit(solution)/shard_map/ppermute | solution.py:382
  134.0 1.6 %collective-permute-done.8 = f32[80,128]{1,0:T(8,128)S(1)} collective-permute-done((f32[80,128]{1,0:T(8,128)S(1)}, f32[80,128]{1,0:T(8,128)S(1)}, u32[]{:S(2)}, u32[]{:S(2)}) %collective-permute-start.8) | collective-permute-done | bytes 40992 | tf_op jit(solution)/shard_map/ppermute | solution.py:382
  135.6 1.7 %collective-permute-start.13 = (f32[80,128]{1,0:T(8,128)S(1)}, f32[80,128]{1,0:T(8,128)S(1)}, u32[]{:S(2)}, u32[]{:S(2)}) collective-permute-start(f32[80,128]{1,0:T(8,128)S(1)} %add_add_fusion.1), channel_id=1, source_target_pairs={{0,4},{1,5},{2,6},{3,7},{4,0},{5,1},{6,2},{7,3},{8,12},{9,13},{10,... | collective-permute-start | bytes 122888 | tf_op jit(solution)/shard_map/ppermute | solution.py:382
  137.4 1.6 %collective-permute-start.12 = (f32[80,128]{1,0:T(8,128)S(1)}, f32[80,128]{1,0:T(8,128)S(1)}, u32[]{:S(2)}, u32[]{:S(2)}) collective-permute-start(f32[80,128]{1,0:T(8,128)S(1)} %add_add_fusion.1), channel_id=1, source_target_pairs={{0,6},{1,7},{2,0},{3,1},{4,2},{5,3},{6,4},{7,5},{8,14},{9,15},{10,... | collective-permute-start | bytes 122888 | tf_op jit(solution)/shard_map/ppermute | solution.py:382
  139.4 1.9 %collective-permute-done.13 = f32[80,128]{1,0:T(8,128)S(1)} collective-permute-done((f32[80,128]{1,0:T(8,128)S(1)}, f32[80,128]{1,0:T(8,128)S(1)}, u32[]{:S(2)}, u32[]{:S(2)}) %collective-permute-start.13) | collective-permute-done | bytes 40992 | tf_op jit(solution)/shard_map/ppermute | solution.py:382
  141.4 2.8 %collective-permute-done.11 = f32[80,128]{1,0:T(8,128)S(1)} collective-permute-done((f32[80,128]{1,0:T(8,128)S(1)}, f32[80,128]{1,0:T(8,128)S(1)}, u32[]{:S(2)}, u32[]{:S(2)}) %collective-permute-start.11) | collective-permute-done | bytes 40992 | tf_op jit(solution)/shard_map/ppermute | solution.py:382
  (68 shorter events, 13.6 us)
Async XLA Ops:
  7.2 94.8 %all-gather.2.cloned.1.call-start = ((), (), s32[]{:S(2)}) async-start(), calls=%async_computation.2 | async-start | bytes 5013504 | tf_op jit(solution)/shard_map/all_gather | solution.py:415
  9.2 5.1 %copy-start.1 = (bf16[1536,2,384]{2,0,1:T(8,128)(2,1)}, bf16[1536,2,384]{2,0,1:T(8,128)(2,1)S(1)}, u32[]{:S(2)}) copy-start(bf16[1536,2,384]{2,0,1:T(8,128)(2,1)S(1)} %copy.27) | copy-start | bytes 7077892
  9.4 1.7 %collective-permute-start = (bf16[12,2,16,384]{3,2,1,0:T(8,128)(2,1)S(1)}, bf16[12,2,16,384]{3,2,1,0:T(8,128)(2,1)S(1)}, u32[]{:S(2)}, u32[]{:S(2)}) collective-permute-start(bf16[12,2,16,384]{3,2,1,0:T(8,128)(2,1)S(1)} %copy.23), channel_id=1, source_target_pairs={{0,1},{1,0},{2,3},{3,2},{4,5},{5,4},{6,7},{7,6},{8,9},{9,8},{10,11... | collective-permute-start | bytes 884744 | tf_op jit(solution)/shard_map/ppermute | solution.py:410
  9.5 5.1 %copy-start.8 = (s32[9,3]{0,1:T(4,128)S(1)}, s32[9,3]{0,1:T(4,128)}, u32[]{:S(2)}) copy-start(s32[9,3]{0,1:T(4,128)} %param.12) | copy-start | bytes 328
  11.1 23.1 %copy-start = (bf16[24,2,16,384]{3,2,1,0:T(8,128)(2,1)}, bf16[24,2,16,384]{3,2,1,0:T(8,128)(2,1)S(1)}, u32[]{:S(2)}) copy-start(bf16[24,2,16,384]{3,2,1,0:T(8,128)(2,1)S(1)} %maximum_select_fusion.tau_ref) | copy-start | bytes 1769476
  14.4 4.7 %collective-permute-start.1 = (bf16[2,1536,384]{2,1,0:T(8,128)(2,1)S(1)}, bf16[2,1536,384]{2,1,0:T(8,128)(2,1)}, u32[]{:S(2)}, u32[]{:S(2)}) collective-permute-start(bf16[2,1536,384]{2,1,0:T(8,128)(2,1)S(1)} %bitcast.25), channel_id=1, source_target_pairs={{0,1},{1,0},{2,3},{3,2},{4,5},{5,4},{6,7},{7,6},{8,9},{9,8},{10,11... | collective-permute-start | bytes 7077896 | tf_op jit(solution)/shard_map/ppermute | solution.py:408
  34.2 33.3 %all-to-all-start = ((bf16[16,24,1664]{2,1,0:T(8,128)(2,1)}), bf16[16,24,1664]{2,1,0:T(8,128)(2,1)S(1)}, u32[]{:S(2)}, u32[]{:S(2)}) async-start(bf16[16,24,1664]{2,1,0:T(8,128)(2,1)} %phase_0.1), calls=%async_computation | async-start | bytes 2555904 | tf_op jit(solution)/shard_map/all_to_all | solution.py:387
  60.0 14.5 %copy-start.9 = (s32[64]{0:T(128)S(1)}, s32[64]{0:T(128)}, u32[]{:S(2)}) copy-start(s32[64]{0:T(128)} %param.13) | copy-start | bytes 772
  60.0 15.2 %copy-start.10 = (s32[64]{0:T(128)S(1)}, s32[64]{0:T(128)}, u32[]{:S(2)}) copy-start(s32[64]{0:T(128)} %param.14) | copy-start | bytes 772
  60.0 15.9 %copy-start.7 = (f32[2,64,8]{1,2,0:T(8,128)S(1)}, f32[2,64,8]{1,2,0:T(8,128)}, u32[]{:S(2)}) copy-start(f32[2,64,8]{1,2,0:T(8,128)} %param.15) | copy-start | bytes 12292
  67.5 31.4 %all-to-all-start.1 = ((bf16[16,24,2048]{2,1,0:T(8,128)(2,1)}), bf16[16,24,2048]{2,1,0:T(8,128)(2,1)S(1)}, u32[]{:S(2)}, u32[]{:S(2)}) async-start(bf16[16,24,2048]{2,1,0:T(8,128)(2,1)} %phase_2.1), calls=%async_computation.1 | async-start | bytes 3145728 | tf_op jit(solution)/shard_map/all_to_all | solution.py:387
  99.6 2.4 %copy-start.2 = (bf16[24,1920]{1,0:T(8,128)(2,1)}, bf16[24,1920]{1,0:T(8,128)(2,1)S(1)}, u32[]{:S(2)}) copy-start(bf16[24,1920]{1,0:T(8,128)(2,1)S(1)} %fusion.own2) | copy-start | bytes 276484
  99.6 2.3 %collective-permute-start.3 = (bf16[24,1920]{1,0:T(8,128)(2,1)S(1)}, bf16[24,1920]{1,0:T(8,128)(2,1)S(1)}, u32[]{:S(2)}, u32[]{:S(2)}) collective-permute-start(bf16[24,1920]{1,0:T(8,128)(2,1)S(1)} %fusion.own2), channel_id=1, source_target_pairs={{0,1},{1,0},{2,3},{3,2},{4,5},{5,4},{6,7},{7,6},{8,9},{9,8},{10,11... | collective-permute-start | bytes 276488 | tf_op jit(solution)/shard_map/ppermute | solution.py:429
  100.3 1.7 %collective-permute-start.2 = (bf16[24,1536]{1,0:T(8,128)(2,1)S(1)}, bf16[24,1536]{1,0:T(8,128)(2,1)S(1)}, u32[]{:S(2)}, u32[]{:S(2)}) collective-permute-start(bf16[24,1536]{1,0:T(8,128)(2,1)S(1)} %fusion.1.own1), channel_id=1, source_target_pairs={{0,1},{1,0},{2,3},{3,2},{4,5},{5,4},{6,7},{7,6},{8,9},{9,8},{10,11... | collective-permute-start | bytes 221192 | tf_op jit(solution)/shard_map/ppermute | solution.py:428
  116.7 1.5 collective-permute-start.4
  118.9 7.7 %collective-permute-start.7 = (f32[8,128]{1,0:T(8,128)S(1)}, f32[8,128]{1,0:T(8,128)S(1)}, u32[]{:S(2)}, u32[]{:S(2)}) collective-permute-start(f32[8,128]{1,0:T(8,128)S(1)} %slice.89), channel_id=1, source_target_pairs={{0,64},{1,65},{2,66},{3,67},{4,68},{5,69},{6,70},{7,71},{8,72},{9,... | collective-permute-start | bytes 12296 | tf_op jit(solution)/shard_map/ppermute | solution.py:435
  124.1 2.6 %collective-permute-start.6 = (f32[8,128]{1,0:T(8,128)S(1)}, f32[8,128]{1,0:T(8,128)S(1)}, u32[]{:S(2)}, u32[]{:S(2)}) collective-permute-start(f32[8,128]{1,0:T(8,128)S(1)} %slice.89), channel_id=1, source_target_pairs={{0,96},{1,97},{2,98},{3,99},{4,100},{5,101},{6,102},{7,103},{8,104... | collective-permute-start | bytes 12296 | tf_op jit(solution)/shard_map/ppermute | solution.py:435
  125.4 2.6 %collective-permute-start.5 = (f32[8,128]{1,0:T(8,128)S(1)}, f32[8,128]{1,0:T(8,128)S(1)}, u32[]{:S(2)}, u32[]{:S(2)}) collective-permute-start(f32[8,128]{1,0:T(8,128)S(1)} %slice.89), channel_id=1, source_target_pairs={{0,32},{1,33},{2,34},{3,35},{4,36},{5,37},{6,38},{7,39},{8,40},{9,... | collective-permute-start | bytes 12296 | tf_op jit(solution)/shard_map/ppermute | solution.py:435
  128.0 6.0 %collective-permute-start.10 = (f32[80,128]{1,0:T(8,128)S(1)}, f32[80,128]{1,0:T(8,128)S(1)}, u32[]{:S(2)}, u32[]{:S(2)}) collective-permute-start(f32[80,128]{1,0:T(8,128)S(1)} %pad_maximum_fusion), channel_id=1, source_target_pairs={{0,16},{1,17},{2,18},{3,19},{4,20},{5,21},{6,22},{7,23},{8,24},{9,... | collective-permute-start | bytes 122888 | tf_op jit(solution)/shard_map/ppermute | solution.py:382
  129.7 4.3 %collective-permute-start.9 = (f32[80,128]{1,0:T(8,128)S(1)}, f32[80,128]{1,0:T(8,128)S(1)}, u32[]{:S(2)}, u32[]{:S(2)}) collective-permute-start(f32[80,128]{1,0:T(8,128)S(1)} %pad_maximum_fusion), channel_id=1, source_target_pairs={{0,24},{1,25},{2,26},{3,27},{4,28},{5,29},{6,30},{7,31},{8,0},{9,1... | collective-permute-start | bytes 122888 | tf_op jit(solution)/shard_map/ppermute | solution.py:382
  130.4 5.2 %collective-permute-start.8 = (f32[80,128]{1,0:T(8,128)S(1)}, f32[80,128]{1,0:T(8,128)S(1)}, u32[]{:S(2)}, u32[]{:S(2)}) collective-permute-start(f32[80,128]{1,0:T(8,128)S(1)} %pad_maximum_fusion), channel_id=1, source_target_pairs={{0,8},{1,9},{2,10},{3,11},{4,12},{5,13},{6,14},{7,15},{8,16},{9,17... | collective-permute-start | bytes 122888 | tf_op jit(solution)/shard_map/ppermute | solution.py:382
  135.6 5.7 %collective-permute-start.13 = (f32[80,128]{1,0:T(8,128)S(1)}, f32[80,128]{1,0:T(8,128)S(1)}, u32[]{:S(2)}, u32[]{:S(2)}) collective-permute-start(f32[80,128]{1,0:T(8,128)S(1)} %add_add_fusion.1), channel_id=1, source_target_pairs={{0,4},{1,5},{2,6},{3,7},{4,0},{5,1},{6,2},{7,3},{8,12},{9,13},{10,... | collective-permute-start | bytes 122888 | tf_op jit(solution)/shard_map/ppermute | solution.py:382
  137.4 4.0 %collective-permute-start.12 = (f32[80,128]{1,0:T(8,128)S(1)}, f32[80,128]{1,0:T(8,128)S(1)}, u32[]{:S(2)}, u32[]{:S(2)}) collective-permute-start(f32[80,128]{1,0:T(8,128)S(1)} %add_add_fusion.1), channel_id=1, source_target_pairs={{0,6},{1,7},{2,0},{3,1},{4,2},{5,3},{6,4},{7,5},{8,14},{9,15},{10,... | collective-permute-start | bytes 122888 | tf_op jit(solution)/shard_map/ppermute | solution.py:382
  139.0 5.2 %collective-permute-start.11 = (f32[80,128]{1,0:T(8,128)S(1)}, f32[80,128]{1,0:T(8,128)S(1)}, u32[]{:S(2)}, u32[]{:S(2)}) collective-permute-start(f32[80,128]{1,0:T(8,128)S(1)} %add_add_fusion.1), channel_id=1, source_target_pairs={{0,2},{1,3},{2,4},{3,5},{4,6},{5,7},{6,0},{7,1},{8,10},{9,11},{10,... | collective-permute-start | bytes 122888 | tf_op jit(solution)/shard_map/ppermute | solution.py:382
  (4 other events, 5.0 us)
Sparse Core Ops, SparseCore 0:
  14.5 73.6 all-gather.1

commit v4 on v3

--- a/solution.py
+++ b/solution.py
@@ -279,11 +279,11 @@
         one = jnp.where(core == c, own1[...], oth1[...]).astype(F32)
         two = jnp.where(core == c, own2[...], oth2[...]).astype(F32)
         for u in range(4):
-            part = one if u < 2 else two
+            part = one if u < 1 else two
             for q in range(2):
-                at = 768 * (u % 2) + 384 * q
+                at = 768 * max(u - 1, 0) + 384 * q
                 rows_ref[q, :, 4 * c + u, :] = part[:, at : at + 384]
-        rows_ref[c, :, 8, :] = two[:, 1536:1920]
+        rows_ref[c, :, 8, :] = one[:, 768:1152]
     real = rows_ref[0].reshape(384, 384).astype(BF)
     imag = rows_ref[1].reshape(384, 384).astype(BF)
     stacked = jnp.concatenate(
@@ -414,11 +414,12 @@
     part = jnp.where(core == 0, tau[..., :192], tau[..., 192:]).reshape(ROWS, 6144)
     tau_all = lax.all_gather(part, "gx", axis=0, tiled=True, axis_index_groups=SAME_CORE)
     flat = momenta.reshape(-1)
-    first = phase_part(own, other, where, flat, 2, 2, 1)
-    got2 = exchanged(first)
-    second = phase_part(own, other, where, flat, 0, 2, 0)
+    first = phase_part(own, other, where, flat, 0, 1, 1)
+    own, first = lax.optimization_barrier((own, first))
+    got1 = exchanged(first)
+    second = phase_part(own, other, where, flat, 1, 3, 0)
     tau, second = lax.optimization_barrier((tau, second))
-    got1 = exchanged(second)
+    got2 = exchanged(second)
     src, left, right, basis = source_part(
         tau, source_blocks, op_momentum, op_gamma, ref_vectors, where
     )

time: 155 us -> 151 us (0.974)
  waiting for transfers between devices: 37.5 us -> 32.1 us
    ppermute x1, waiting for transfers between devices: 3.84 us -> 0.01 us  [body(): other = lax.ppermute(own, 'gx', PAIR)]
    ppermute x6, waiting for transfers between devices: 8.69 us -> 5.9 us  [around(): sent = [lax.ppermute(shard, 'gx', shift(*axis * d)) for d in (1, 3, 2)]]
    all_to_all x2, waiting for transfers between devices: 20.1 us -> 21.8 us  [exchanged(): lax.all_to_all(part, 'gx', 0, 0, tiled=True, axis_index_groups=SAME_CORE)]
    ppermute x6, starting transfers between devices: 7.49 us -> 9.17 us  [around(): sent = [lax.ppermute(shard, 'gx', shift(*axis * d)) for d in (1, 3, 2)]]
  transfers between devices with their start and end apart: 17 -> 17, of which waited for: 12 -> 9; matrix products, arithmetic and copies ran while one was open for 3% -> 5% of each run, Pallas kernels for 28% -> 28%
where the time goes in v4:
time: 151 us; the launch traced here: 149 us
  Pallas kernels  56.6 us (37%)
  starting transfers between devices  32.8 us (22%)
  waiting for transfers between devices  32.1 us (21%)
  between operations  15 us (10%)
  local copies, waits for them, and re-layouts  8.42 us (6%)
  other arithmetic  4.5 us (3%)
    pallas_call x2, Pallas kernels, phase_part(): pl.pallas_call(functools.partial(phase_kernel, first, full, half, steps),...  33 us
    all_to_all x2, waiting for transfers between devices, exchanged(): lax.all_to_all(part, 'gx', 0, 0, tiled=True, axis_index_groups=SAME_CORE)  21.8 us
    all_to_all x2, starting transfers between devices, exchanged(): lax.all_to_all(part, 'gx', 0, 0, tiled=True, axis_index_groups=SAME_CORE)  15.3 us
    pallas_call x1, Pallas kernels, sink_part(): pl.pallas_call(sink_kernel, grid_spec=pltpu.PrefetchScalarGridSpec(num_sc...  14 us
    pallas_call x1, Pallas kernels, source_part(): pl.pallas_call(source_kernel, grid_spec=pltpu.PrefetchScalarGridSpec(num_...  9.6 us
    ppermute x6, starting transfers between devices, around(): sent = [lax.ppermute(shard, 'gx', shift(*axis * d)) for d in (1, 3, 2)]  9.17 us
    ppermute x3, starting transfers between devices, body(): first_raw = first_raw + lax.ppermute(raw, 'ta', [(0, t)])  6.52 us
    ppermute x6, waiting for transfers between devices, around(): sent = [lax.ppermute(shard, 'gx', shift(*axis * d)) for d in (1, 3, 2)]  5.9 us
  transfers between devices with their start and end apart: 17, of which 9 were waited for; matrix products, arithmetic and copies ran while one was open for 5% of the time, Pallas kernels for 28%

profile of v4, /device:TPU:0, one launch (start us, length us, event | category | flops | bytes accessed | tf_op | source)
XLA Modules:
  0.0 149.4 jit_solution(479152771056494244)
XLA Ops:
  7.2 2.0 %copy.27 = bf16[1536,2,384]{2,0,1:T(8,128)(2,1)S(1)} copy(bf16[1536,2,384]{2,1,0:T(2,128)(2,1)} %bitcast.24) | data formatting | bytes 4718592 | tf_op jit(solution)/shard_map/reshape | solution.py:406
  10.0 1.1 collective-permute-done.1
  11.2 1.0 slice_select_fusion
  12.1 2.2 %reshape.50 = bf16[24,6144]{1,0:T(8,128)(2,1)} reshape(bf16[24,2,16,192]{3,2,1,0:T(8,128)(2,1)} %slice_select_fusion) | data formatting | bytes 589824 | tf_op jit(solution)/shard_map/reshape | solution.py:414
  15.1 13.7 %phase_0.1 = bf16[16,24,1280]{2,1,0:T(8,128)(2,1)} custom-call(s32[1]{0:T(128)} %bitcast.where_ref, s32[27]{0:T(128)} %reshape.48.mom_ref, bf16[2,1536,384]{2,1,0:T(8,128)(2,1)} %bitcast.26, bf16[2,1536,384]{2,1,0:T(8,128)(2,1)} %collective-permute-done.other_ref), custom_call_target="tpu_custom_call" | custom-call | flops 10871635968 | bytes 6291456 | tf_op jit(solution)/shard_map/phase_0/pallas_call | solution.py:157
  28.8 8.0 %all-to-all-start = ((bf16[16,24,1280]{2,1,0:T(8,128)(2,1)}), bf16[16,24,1280]{2,1,0:T(8,128)(2,1)S(1)}, u32[]{:S(2)}, u32[]{:S(2)}) async-start(bf16[16,24,1280]{2,1,0:T(8,128)(2,1)} %phase_0.1), calls=%async_computation | async-start | bytes 1966080 | tf_op jit(solution)/shard_map/all_to_all | solution.py:387
  36.7 19.3 %phase_1.1 = bf16[16,24,2432]{2,1,0:T(8,128)(2,1)} custom-call(s32[1]{0:T(128)} %bitcast.where_ref, s32[27]{0:T(128)} %reshape.48.mom_ref, bf16[2,1536,384]{2,1,0:T(8,128)(2,1)} %bitcast.27, bf16[2,1536,384]{2,1,0:T(8,128)(2,1)} %collective-permute-done.other_ref), custom_call_target="tpu_custom_call" | custom-call | flops 21743271936 | bytes 6291456 | tf_op jit(solution)/shard_map/phase_1/pallas_call | solution.py:157
  56.0 7.3 %all-to-all-start.1 = ((bf16[16,24,2432]{2,1,0:T(8,128)(2,1)}), bf16[16,24,2432]{2,1,0:T(8,128)(2,1)S(1)}, u32[]{:S(2)}, u32[]{:S(2)}) async-start(bf16[16,24,2432]{2,1,0:T(8,128)(2,1)} %phase_1.1), calls=%async_computation.1 | async-start | bytes 3735552 | tf_op jit(solution)/shard_map/all_to_all | solution.py:387
  65.5 9.6 %source.1 = (bf16[24,2,9,16,192]{4,3,2,1,0:T(8,128)(2,1)}, f32[2,256,64]{2,1,0:T(8,128)}, f32[2,4,64,144]{3,2,1,0:T(8,128)}, f32[2,64,8]{2,1,0:T(8,128)}) custom-call(s32[1]{0:T(128)} %bitcast.where_ref, bf16[24,2,16,384]{3,2,1,0:T(8,128)(2,1)} %copy-done, bf16[9,2,384,384]{3,2,1,0:T(8,128)(2,1)} %src_ref.1, s32[64,1]{1,0:T(8,128)} %copy.20.mom_ref, ...), custom_call_target="tpu_custom_call" | custom-call | flops 2038431744 | bytes 8388608 | tf_op jit(solution)/shard_map/source/pallas_call | solution.py:212
  75.1 21.8 %all-to-all-done.1 = bf16[16,24,2432]{2,1,0:T(8,128)(2,1)S(1)} async-done(((bf16[16,24,2432]{2,1,0:T(8,128)(2,1)}), bf16[16,24,2432]{2,1,0:T(8,128)(2,1)S(1)}, u32[]{:S(2)}, u32[]{:S(2)}) %all-to-all-start.1) | async-done | bytes 1867808 | tf_op jit(solution)/shard_map/all_to_all | solution.py:387
  99.0 0.9 collective-permute-done.2.oth1
  100.6 14.0 %sink.1 = f32[72,128]{1,0:T(8,128)} custom-call(s32[1]{0:T(128)} %bitcast.where_ref, bf16[24,1152]{1,0:T(8,128)(2,1)} %copy-done.4, bf16[24,1152]{1,0:T(8,128)(2,1)} %copy-done.6, bf16[24,2304]{1,0:T(8,128)(2,1)} %copy-done.2, bf16[24,2304]{1,0:T(8,128)(2,1)} %copy-done.5, bf16[384,6144]{1,0:T(8,128)(2,1)} %all-gather.2.cloned.1.call-done.tau_hbm, ...), custom_call_target="tpu_custom_call" | custom-call | tf_op jit(solution)/shard_map/sink/pallas_call | solution.py:359
  115.1 1.1 collective-permute-done.4
  116.9 3.3 %collective-permute-start.5 = (f32[8,128]{1,0:T(8,128)S(1)}, f32[8,128]{1,0:T(8,128)S(1)}, u32[]{:S(2)}, u32[]{:S(2)}) collective-permute-start(f32[8,128]{1,0:T(8,128)S(1)} %slice.89), channel_id=1, source_target_pairs={{0,32},{1,33},{2,34},{3,35},{4,36},{5,37},{6,38},{7,39},{8,40},{9,... | collective-permute-start | bytes 12296 | tf_op jit(solution)/shard_map/ppermute | solution.py:436
  120.3 1.9 %collective-permute-start.6 = (f32[8,128]{1,0:T(8,128)S(1)}, f32[8,128]{1,0:T(8,128)S(1)}, u32[]{:S(2)}, u32[]{:S(2)}) collective-permute-start(f32[8,128]{1,0:T(8,128)S(1)} %slice.89), channel_id=1, source_target_pairs={{0,96},{1,97},{2,98},{3,99},{4,100},{5,101},{6,102},{7,103},{8,104... | collective-permute-start | bytes 12296 | tf_op jit(solution)/shard_map/ppermute | solution.py:436
  122.2 1.3 collective-permute-start.7
  123.5 1.3 collective-permute-done.7
  124.8 1.1 collective-permute-start.10
  125.8 1.0 collective-permute-start.8
  126.8 2.2 %collective-permute-start.9 = (f32[80,128]{1,0:T(8,128)S(1)}, f32[80,128]{1,0:T(8,128)S(1)}, u32[]{:S(2)}, u32[]{:S(2)}) collective-permute-start(f32[80,128]{1,0:T(8,128)S(1)} %pad_maximum_fusion), channel_id=1, source_target_pairs={{0,24},{1,25},{2,26},{3,27},{4,28},{5,29},{6,30},{7,31},{8,0},{9,1... | collective-permute-start | bytes 122888 | tf_op jit(solution)/shard_map/ppermute | solution.py:382
  129.1 1.3 collective-permute-done.10
  131.8 2.5 %collective-permute-start.12 = (f32[80,128]{1,0:T(8,128)S(1)}, f32[80,128]{1,0:T(8,128)S(1)}, u32[]{:S(2)}, u32[]{:S(2)}) collective-permute-start(f32[80,128]{1,0:T(8,128)S(1)} %add_add_fusion.1), channel_id=1, source_target_pairs={{0,6},{1,7},{2,0},{3,1},{4,2},{5,3},{6,4},{7,5},{8,14},{9,15},{10,... | collective-permute-start | bytes 122888 | tf_op jit(solution)/shard_map/ppermute | solution.py:382
  134.4 1.6 %collective-permute-start.13 = (f32[80,128]{1,0:T(8,128)S(1)}, f32[80,128]{1,0:T(8,128)S(1)}, u32[]{:S(2)}, u32[]{:S(2)}) collective-permute-start(f32[80,128]{1,0:T(8,128)S(1)} %add_add_fusion.1), channel_id=1, source_target_pairs={{0,4},{1,5},{2,6},{3,7},{4,0},{5,1},{6,2},{7,3},{8,12},{9,13},{10,... | collective-permute-start | bytes 122888 | tf_op jit(solution)/shard_map/ppermute | solution.py:382
  136.8 3.1 %collective-permute-done.13 = f32[80,128]{1,0:T(8,128)S(1)} collective-permute-done((f32[80,128]{1,0:T(8,128)S(1)}, f32[80,128]{1,0:T(8,128)S(1)}, u32[]{:S(2)}, u32[]{:S(2)}) %collective-permute-start.13) | collective-permute-done | bytes 40992 | tf_op jit(solution)/shard_map/ppermute | solution.py:382
  (69 shorter events, 11.9 us)
Async XLA Ops:
  7.2 92.8 %all-gather.2.cloned.1.call-start = ((), (), s32[]{:S(2)}) async-start(), calls=%async_computation.2 | async-start | bytes 5013504 | tf_op jit(solution)/shard_map/all_gather | solution.py:415
  9.2 5.1 %copy-start.1 = (bf16[1536,2,384]{2,0,1:T(8,128)(2,1)}, bf16[1536,2,384]{2,0,1:T(8,128)(2,1)S(1)}, u32[]{:S(2)}) copy-start(bf16[1536,2,384]{2,0,1:T(8,128)(2,1)S(1)} %copy.27) | copy-start | bytes 7077892
  9.3 5.0 %copy-start.8 = (s32[9,3]{0,1:T(4,128)S(1)}, s32[9,3]{0,1:T(4,128)}, u32[]{:S(2)}) copy-start(s32[9,3]{0,1:T(4,128)} %param.12) | copy-start | bytes 328
  9.4 1.7 %collective-permute-start.1 = (bf16[12,2,16,384]{3,2,1,0:T(8,128)(2,1)S(1)}, bf16[12,2,16,384]{3,2,1,0:T(8,128)(2,1)S(1)}, u32[]{:S(2)}, u32[]{:S(2)}) collective-permute-start(bf16[12,2,16,384]{3,2,1,0:T(8,128)(2,1)S(1)} %copy.23), channel_id=1, source_target_pairs={{0,1},{1,0},{2,3},{3,2},{4,5},{5,4},{6,7},{7,6},{8,9},{9,8},{10,11... | collective-permute-start | bytes 884744 | tf_op jit(solution)/shard_map/ppermute | solution.py:410
  9.5 5.6 %collective-permute-start = (bf16[2,1536,384]{2,1,0:T(8,128)(2,1)S(1)}, bf16[2,1536,384]{2,1,0:T(8,128)(2,1)}, u32[]{:S(2)}, u32[]{:S(2)}) collective-permute-start(bf16[2,1536,384]{2,1,0:T(8,128)(2,1)S(1)} %bitcast.25), channel_id=1, source_target_pairs={{0,1},{1,0},{2,3},{3,2},{4,5},{5,4},{6,7},{7,6},{8,9},{9,8},{10,11... | collective-permute-start | bytes 7077896 | tf_op jit(solution)/shard_map/ppermute | solution.py:408
  11.2 17.6 %copy-start = (bf16[24,2,16,384]{3,2,1,0:T(8,128)(2,1)}, bf16[24,2,16,384]{3,2,1,0:T(8,128)(2,1)S(1)}, u32[]{:S(2)}) copy-start(bf16[24,2,16,384]{3,2,1,0:T(8,128)(2,1)S(1)} %maximum_select_fusion.tau_ref) | copy-start | bytes 1769476
  28.8 27.2 %all-to-all-start = ((bf16[16,24,1280]{2,1,0:T(8,128)(2,1)}), bf16[16,24,1280]{2,1,0:T(8,128)(2,1)S(1)}, u32[]{:S(2)}, u32[]{:S(2)}) async-start(bf16[16,24,1280]{2,1,0:T(8,128)(2,1)} %phase_0.1), calls=%async_computation | async-start | bytes 1966080 | tf_op jit(solution)/shard_map/all_to_all | solution.py:387
  56.0 7.3 %copy-start.7 = (f32[2,64,8]{1,2,0:T(8,128)S(1)}, f32[2,64,8]{1,2,0:T(8,128)}, u32[]{:S(2)}) copy-start(f32[2,64,8]{1,2,0:T(8,128)} %param.15) | copy-start | bytes 12292
  56.0 8.1 %copy-start.9 = (s32[64]{0:T(128)S(1)}, s32[64]{0:T(128)}, u32[]{:S(2)}) copy-start(s32[64]{0:T(128)} %param.13) | copy-start | bytes 772
  56.0 8.8 %copy-start.10 = (s32[64]{0:T(128)S(1)}, s32[64]{0:T(128)}, u32[]{:S(2)}) copy-start(s32[64]{0:T(128)} %param.14) | copy-start | bytes 772
  56.0 40.9 %all-to-all-start.1 = ((bf16[16,24,2432]{2,1,0:T(8,128)(2,1)}), bf16[16,24,2432]{2,1,0:T(8,128)(2,1)S(1)}, u32[]{:S(2)}, u32[]{:S(2)}) async-start(bf16[16,24,2432]{2,1,0:T(8,128)(2,1)} %phase_1.1), calls=%async_computation.1 | async-start | bytes 3735552 | tf_op jit(solution)/shard_map/all_to_all | solution.py:387
  97.7 2.3 %copy-start.2 = (bf16[24,2304]{1,0:T(8,128)(2,1)}, bf16[24,2304]{1,0:T(8,128)(2,1)S(1)}, u32[]{:S(2)}) copy-start(bf16[24,2304]{1,0:T(8,128)(2,1)S(1)} %fusion.own2) | copy-start | bytes 331780
  97.7 2.2 %collective-permute-start.3 = (bf16[24,2304]{1,0:T(8,128)(2,1)S(1)}, bf16[24,2304]{1,0:T(8,128)(2,1)S(1)}, u32[]{:S(2)}, u32[]{:S(2)}) collective-permute-start(bf16[24,2304]{1,0:T(8,128)(2,1)S(1)} %fusion.own2), channel_id=1, source_target_pairs={{0,1},{1,0},{2,3},{3,2},{4,5},{5,4},{6,7},{7,6},{8,9},{9,8},{10,11... | collective-permute-start | bytes 331784 | tf_op jit(solution)/shard_map/ppermute | solution.py:430
  98.3 1.6 %collective-permute-start.2 = (bf16[24,1152]{1,0:T(8,128)(2,1)S(1)}, bf16[24,1152]{1,0:T(8,128)(2,1)S(1)}, u32[]{:S(2)}, u32[]{:S(2)}) collective-permute-start(bf16[24,1152]{1,0:T(8,128)(2,1)S(1)} %fusion.1.own1), channel_id=1, source_target_pairs={{0,1},{1,0},{2,3},{3,2},{4,5},{5,4},{6,7},{7,6},{8,9},{9,8},{10,11... | collective-permute-start | bytes 165896 | tf_op jit(solution)/shard_map/ppermute | solution.py:429
  114.6 1.5 %collective-permute-start.4 = (f32[72,128]{1,0:T(8,128)}, f32[72,128]{1,0:T(8,128)S(1)}, u32[]{:S(2)}, u32[]{:S(2)}) collective-permute-start(f32[72,128]{1,0:T(8,128)} %sink.1), channel_id=1, source_target_pairs={{0,1},{1,0},{2,3},{3,2},{4,5},{5,4},{6,7},{7,6},{8,9},{9,8},{10,11... | collective-permute-start | bytes 110600 | tf_op jit(solution)/shard_map/ppermute | solution.py:432
  116.9 6.6 %collective-permute-start.5 = (f32[8,128]{1,0:T(8,128)S(1)}, f32[8,128]{1,0:T(8,128)S(1)}, u32[]{:S(2)}, u32[]{:S(2)}) collective-permute-start(f32[8,128]{1,0:T(8,128)S(1)} %slice.89), channel_id=1, source_target_pairs={{0,32},{1,33},{2,34},{3,35},{4,36},{5,37},{6,38},{7,39},{8,40},{9,... | collective-permute-start | bytes 12296 | tf_op jit(solution)/shard_map/ppermute | solution.py:436
  120.3 3.2 %collective-permute-start.6 = (f32[8,128]{1,0:T(8,128)S(1)}, f32[8,128]{1,0:T(8,128)S(1)}, u32[]{:S(2)}, u32[]{:S(2)}) collective-permute-start(f32[8,128]{1,0:T(8,128)S(1)} %slice.89), channel_id=1, source_target_pairs={{0,96},{1,97},{2,98},{3,99},{4,100},{5,101},{6,102},{7,103},{8,104... | collective-permute-start | bytes 12296 | tf_op jit(solution)/shard_map/ppermute | solution.py:436
  122.2 2.6 %collective-permute-start.7 = (f32[8,128]{1,0:T(8,128)S(1)}, f32[8,128]{1,0:T(8,128)S(1)}, u32[]{:S(2)}, u32[]{:S(2)}) collective-permute-start(f32[8,128]{1,0:T(8,128)S(1)} %slice.89), channel_id=1, source_target_pairs={{0,64},{1,65},{2,66},{3,67},{4,68},{5,69},{6,70},{7,71},{8,72},{9,... | collective-permute-start | bytes 12296 | tf_op jit(solution)/shard_map/ppermute | solution.py:436
  124.8 5.6 %collective-permute-start.10 = (f32[80,128]{1,0:T(8,128)S(1)}, f32[80,128]{1,0:T(8,128)S(1)}, u32[]{:S(2)}, u32[]{:S(2)}) collective-permute-start(f32[80,128]{1,0:T(8,128)S(1)} %pad_maximum_fusion), channel_id=1, source_target_pairs={{0,16},{1,17},{2,18},{3,19},{4,20},{5,21},{6,22},{7,23},{8,24},{9,... | collective-permute-start | bytes 122888 | tf_op jit(solution)/shard_map/ppermute | solution.py:382
  125.8 5.2 %collective-permute-start.8 = (f32[80,128]{1,0:T(8,128)S(1)}, f32[80,128]{1,0:T(8,128)S(1)}, u32[]{:S(2)}, u32[]{:S(2)}) collective-permute-start(f32[80,128]{1,0:T(8,128)S(1)} %pad_maximum_fusion), channel_id=1, source_target_pairs={{0,8},{1,9},{2,10},{3,11},{4,12},{5,13},{6,14},{7,15},{8,16},{9,17... | collective-permute-start | bytes 122888 | tf_op jit(solution)/shard_map/ppermute | solution.py:382
  126.8 4.2 %collective-permute-start.9 = (f32[80,128]{1,0:T(8,128)S(1)}, f32[80,128]{1,0:T(8,128)S(1)}, u32[]{:S(2)}, u32[]{:S(2)}) collective-permute-start(f32[80,128]{1,0:T(8,128)S(1)} %pad_maximum_fusion), channel_id=1, source_target_pairs={{0,24},{1,25},{2,26},{3,27},{4,28},{5,29},{6,30},{7,31},{8,0},{9,1... | collective-permute-start | bytes 122888 | tf_op jit(solution)/shard_map/ppermute | solution.py:382
  131.1 5.7 %collective-permute-start.11 = (f32[80,128]{1,0:T(8,128)S(1)}, f32[80,128]{1,0:T(8,128)S(1)}, u32[]{:S(2)}, u32[]{:S(2)}) collective-permute-start(f32[80,128]{1,0:T(8,128)S(1)} %add_add_fusion.1), channel_id=1, source_target_pairs={{0,2},{1,3},{2,4},{3,5},{4,6},{5,7},{6,0},{7,1},{8,10},{9,11},{10,... | collective-permute-start | bytes 122888 | tf_op jit(solution)/shard_map/ppermute | solution.py:382
  131.8 5.0 %collective-permute-start.12 = (f32[80,128]{1,0:T(8,128)S(1)}, f32[80,128]{1,0:T(8,128)S(1)}, u32[]{:S(2)}, u32[]{:S(2)}) collective-permute-start(f32[80,128]{1,0:T(8,128)S(1)} %add_add_fusion.1), channel_id=1, source_target_pairs={{0,6},{1,7},{2,0},{3,1},{4,2},{5,3},{6,4},{7,5},{8,14},{9,15},{10,... | collective-permute-start | bytes 122888 | tf_op jit(solution)/shard_map/ppermute | solution.py:382
  134.4 5.5 %collective-permute-start.13 = (f32[80,128]{1,0:T(8,128)S(1)}, f32[80,128]{1,0:T(8,128)S(1)}, u32[]{:S(2)}, u32[]{:S(2)}) collective-permute-start(f32[80,128]{1,0:T(8,128)S(1)} %add_add_fusion.1), channel_id=1, source_target_pairs={{0,4},{1,5},{2,6},{3,7},{4,0},{5,1},{6,2},{7,3},{8,12},{9,13},{10,... | collective-permute-start | bytes 122888 | tf_op jit(solution)/shard_map/ppermute | solution.py:382
  (4 other events, 5.0 us)
Sparse Core Ops, SparseCore 0:
  14.5 71.5 all-gather.1

commit v5 on v4

--- a/solution.py
+++ b/solution.py
@@ -308,7 +308,7 @@
         acc_ref[...] += dot(right, left, 1, 1)
         return carry
 
-    lax.fori_loop(0, ROWS, one_row, 0, unroll=8)
+    lax.fori_loop(0, ROWS, one_row, 0, unroll=12)
     acc = acc_ref[...]
     block_real = acc[:144, :256] - acc[144:, 256:]
     block_imag = acc[144:, :256] + acc[:144, 256:]
@@ -403,9 +403,10 @@
     device = lax.axis_index("gx")
     core = device % 2
     where = device[None]
-    own = jnp.transpose(eigvecs.reshape(-1, 2, 384), (1, 0, 2))
+    mixed = eigvecs.reshape(-1, 2, 384)
+    own = jnp.transpose(mixed, (1, 0, 2))
+    other = jnp.transpose(lax.ppermute(mixed, "gx", PAIR), (1, 0, 2))
     own, perambulators = lax.optimization_barrier((own, perambulators))
-    other = lax.ppermute(own, "gx", PAIR)
     mine = jnp.transpose(perambulators[0], (1, 0, 2, 3, 4)).reshape(12, 2, 16, 384)
     theirs = lax.ppermute(mine, "gx", PAIR)
     tau = jnp.where(
@@ -423,10 +424,10 @@
     src, left, right, basis = source_part(
         tau, source_blocks, op_momentum, op_gamma, ref_vectors, where
     )
-    got1, got2, src = lax.optimization_barrier((got1, got2, src))
     own1 = summed(got1, device // 2)
+    oth1 = lax.ppermute(own1, "gx", PAIR)
+    got2, src, oth1 = lax.optimization_barrier((got2, src, oth1))
     own2 = summed(got2, device // 2)
-    oth1 = lax.ppermute(own1, "gx", PAIR)
     oth2 = lax.ppermute(own2, "gx", PAIR)
     corr = sink_part(where, own1, oth1, own2, oth2, tau_all, src, left, right, basis)
     corr = corr + lax.ppermute(corr, "gx", PAIR)

time: 151 us -> 151 us (level)
  waiting for transfers between devices: 32.1 us -> 34.1 us
    ppermute x1, waiting for transfers between devices: 0.01 us -> 3.84 us  [body(): other = jnp.transpose(lax.ppermute(mixed, 'gx', PAIR), (1, 0, 2))]
    all_to_all x2, waiting for transfers between devices: 21.8 us -> 18.3 us  [exchanged(): lax.all_to_all(part, 'gx', 0, 0, tiled=True, axis_index_groups=SAME_CORE)]
  transfers between devices with their start and end apart: 17 -> 17, of which waited for: 9 -> 10; matrix products, arithmetic and copies ran while one was open for 5% -> 3% of each run, Pallas kernels for 28% -> 28%
where the time goes in v5:
time: 151 us; the launch traced here: 149 us
  Pallas kernels  56.3 us (37%)
  waiting for transfers between devices  34.1 us (23%)
  starting transfers between devices  32.8 us (22%)
  between operations  15 us (10%)
  local copies, waits for them, and re-layouts  7.37 us (5%)
  other arithmetic  3.71 us (2%)
    pallas_call x2, Pallas kernels, phase_part(): pl.pallas_call(functools.partial(phase_kernel, first, full, half, steps),...  32.9 us
    all_to_all x2, waiting for transfers between devices, exchanged(): lax.all_to_all(part, 'gx', 0, 0, tiled=True, axis_index_groups=SAME_CORE)  18.3 us
    all_to_all x2, starting transfers between devices, exchanged(): lax.all_to_all(part, 'gx', 0, 0, tiled=True, axis_index_groups=SAME_CORE)  15.3 us
    pallas_call x1, Pallas kernels, sink_part(): pl.pallas_call(sink_kernel, grid_spec=pltpu.PrefetchScalarGridSpec(num_sc...  13.8 us
    ppermute x6, starting transfers between devices, around(): sent = [lax.ppermute(shard, 'gx', shift(*axis * d)) for d in (1, 3, 2)]  9.7 us
    pallas_call x1, Pallas kernels, source_part(): pl.pallas_call(source_kernel, grid_spec=pltpu.PrefetchScalarGridSpec(num_...  9.55 us
    ppermute x3, starting transfers between devices, body(): first_raw = first_raw + lax.ppermute(raw, 'ta', [(0, t)])  6.85 us
    ppermute x6, waiting for transfers between devices, around(): sent = [lax.ppermute(shard, 'gx', shift(*axis * d)) for d in (1, 3, 2)]  6.59 us
  transfers between devices with their start and end apart: 17, of which 10 were waited for; matrix products, arithmetic and copies ran while one was open for 3% of the time, Pallas kernels for 28%

profile of v5, /device:TPU:0, one launch (start us, length us, event | category | flops | bytes accessed | tf_op | source)
XLA Modules:
  0.0 149.3 jit_solution(13801481966876976416)
XLA Ops:
  7.2 2.0 %copy.29 = bf16[1536,2,384]{2,0,1:T(8,128)(2,1)S(1)} copy(bf16[1536,2,384]{2,1,0:T(2,128)(2,1)} %bitcast.24) | data formatting | bytes 4718592 | tf_op jit(solution)/shard_map/reshape | solution.py:406
  9.5 1.6 %collective-permute-done.1 = bf16[12,2,16,384]{3,2,1,0:T(8,128)(2,1)S(1)} collective-permute-done((bf16[12,2,16,384]{3,2,1,0:T(8,128)(2,1)S(1)}, bf16[12,2,16,384]{3,2,1,0:T(8,128)(2,1)S(1)}, u32[]{:S(2)}, u32[]{:S(2)}) %collective-permute-start.1) | collective-permute-done | bytes 294944 | tf_op jit(solution)/shard_map/ppermute | solution.py:411
  11.3 1.1 reshape.50
  13.4 3.8 %collective-permute-done = bf16[1536,2,384]{2,0,1:T(8,128)(2,1)} collective-permute-done((bf16[1536,2,384]{2,0,1:T(8,128)(2,1)S(1)}, bf16[1536,2,384]{2,0,1:T(8,128)(2,1)}, u32[]{:S(2)}, u32[]{:S(2)}) %collective-permute-start) | collective-permute-done | bytes 2359328 | tf_op jit(solution)/shard_map/ppermute | solution.py:408
  17.3 13.7 %phase_0.1 = bf16[16,24,1280]{2,1,0:T(8,128)(2,1)} custom-call(s32[1]{0:T(128)} %bitcast.where_ref, s32[27]{0:T(128)} %reshape.48.mom_ref, bf16[2,1536,384]{2,1,0:T(8,128)(2,1)} %bitcast.25, bf16[2,1536,384]{2,1,0:T(8,128)(2,1)} %bitcast.3.other_ref), custom_call_target="tpu_custom_call" | custom-call | flops 10871635968 | bytes 6291456 | tf_op jit(solution)/shard_map/phase_0/pallas_call | solution.py:157
  30.9 8.0 %all-to-all-start = ((bf16[16,24,1280]{2,1,0:T(8,128)(2,1)}), bf16[16,24,1280]{2,1,0:T(8,128)(2,1)S(1)}, u32[]{:S(2)}, u32[]{:S(2)}) async-start(bf16[16,24,1280]{2,1,0:T(8,128)(2,1)} %phase_0.1), calls=%async_computation | async-start | bytes 1966080 | tf_op jit(solution)/shard_map/all_to_all | solution.py:387
  38.9 19.2 %phase_1.1 = bf16[16,24,2432]{2,1,0:T(8,128)(2,1)} custom-call(s32[1]{0:T(128)} %bitcast.where_ref, s32[27]{0:T(128)} %reshape.48.mom_ref, bf16[2,1536,384]{2,1,0:T(8,128)(2,1)} %bitcast.26, bf16[2,1536,384]{2,1,0:T(8,128)(2,1)} %bitcast.3.other_ref), custom_call_target="tpu_custom_call" | custom-call | flops 21743271936 | bytes 6291456 | tf_op jit(solution)/shard_map/phase_1/pallas_call | solution.py:157
  58.1 7.4 %all-to-all-start.1 = ((bf16[16,24,2432]{2,1,0:T(8,128)(2,1)}), bf16[16,24,2432]{2,1,0:T(8,128)(2,1)S(1)}, u32[]{:S(2)}, u32[]{:S(2)}) async-start(bf16[16,24,2432]{2,1,0:T(8,128)(2,1)} %phase_1.1), calls=%async_computation.1 | async-start | bytes 3735552 | tf_op jit(solution)/shard_map/all_to_all | solution.py:387
  68.3 9.6 %source.1 = (bf16[24,2,9,16,192]{4,3,2,1,0:T(8,128)(2,1)}, f32[2,256,64]{2,1,0:T(8,128)}, f32[2,4,64,144]{3,2,1,0:T(8,128)}, f32[2,64,8]{2,1,0:T(8,128)}) custom-call(s32[1]{0:T(128)} %bitcast.where_ref, bf16[24,2,16,384]{3,2,1,0:T(8,128)(2,1)} %copy-done, bf16[9,2,384,384]{3,2,1,0:T(8,128)(2,1)} %src_ref.1, s32[64,1]{1,0:T(8,128)} %copy.21.mom_ref, ...), custom_call_target="tpu_custom_call" | custom-call | flops 2038431744 | bytes 8388608 | tf_op jit(solution)/shard_map/source/pallas_call | solution.py:212
  77.8 18.3 %all-to-all-done.1 = bf16[16,24,2432]{2,1,0:T(8,128)(2,1)S(1)} async-done(((bf16[16,24,2432]{2,1,0:T(8,128)(2,1)}), bf16[16,24,2432]{2,1,0:T(8,128)(2,1)S(1)}, u32[]{:S(2)}, u32[]{:S(2)}) %all-to-all-start.1) | async-done | bytes 1867808 | tf_op jit(solution)/shard_map/all_to_all | solution.py:387
  97.2 1.3 collective-permute-done.3.oth2
  99.1 13.8 %sink.1 = f32[72,128]{1,0:T(8,128)} custom-call(s32[1]{0:T(128)} %bitcast.where_ref, bf16[24,1152]{1,0:T(8,128)(2,1)} %copy-done.4, bf16[24,1152]{1,0:T(8,128)(2,1)} %copy-done.6, bf16[24,2304]{1,0:T(8,128)(2,1)} %copy-done.2, bf16[24,2304]{1,0:T(8,128)(2,1)} %copy-done.5, bf16[384,6144]{1,0:T(8,128)(2,1)} %all-gather.2.cloned.1.call-done.tau_hbm, ...), custom_call_target="tpu_custom_call" | custom-call | tf_op jit(solution)/shard_map/sink/pallas_call | solution.py:359
  113.2 1.3 collective-permute-done.4
  115.3 3.5 %collective-permute-start.5 = (f32[8,128]{1,0:T(8,128)S(1)}, f32[8,128]{1,0:T(8,128)S(1)}, u32[]{:S(2)}, u32[]{:S(2)}) collective-permute-start(f32[8,128]{1,0:T(8,128)S(1)} %slice.89), channel_id=1, source_target_pairs={{0,32},{1,33},{2,34},{3,35},{4,36},{5,37},{6,38},{7,39},{8,40},{9,... | collective-permute-start | bytes 12296 | tf_op jit(solution)/shard_map/ppermute | solution.py:437
  118.7 2.1 %collective-permute-start.6 = (f32[8,128]{1,0:T(8,128)S(1)}, f32[8,128]{1,0:T(8,128)S(1)}, u32[]{:S(2)}, u32[]{:S(2)}) collective-permute-start(f32[8,128]{1,0:T(8,128)S(1)} %slice.89), channel_id=1, source_target_pairs={{0,96},{1,97},{2,98},{3,99},{4,100},{5,101},{6,102},{7,103},{8,104... | collective-permute-start | bytes 12296 | tf_op jit(solution)/shard_map/ppermute | solution.py:437
  120.8 1.3 collective-permute-start.7
  122.2 1.3 collective-permute-done.7
  123.5 2.3 %collective-permute-start.10 = (f32[80,128]{1,0:T(8,128)S(1)}, f32[80,128]{1,0:T(8,128)S(1)}, u32[]{:S(2)}, u32[]{:S(2)}) collective-permute-start(f32[80,128]{1,0:T(8,128)S(1)} %pad_maximum_fusion), channel_id=1, source_target_pairs={{0,16},{1,17},{2,18},{3,19},{4,20},{5,21},{6,22},{7,23},{8,24},{9,... | collective-permute-start | bytes 122888 | tf_op jit(solution)/shard_map/ppermute | solution.py:382
  125.9 3.0 %collective-permute-start.9 = (f32[80,128]{1,0:T(8,128)S(1)}, f32[80,128]{1,0:T(8,128)S(1)}, u32[]{:S(2)}, u32[]{:S(2)}) collective-permute-start(f32[80,128]{1,0:T(8,128)S(1)} %pad_maximum_fusion), channel_id=1, source_target_pairs={{0,24},{1,25},{2,26},{3,27},{4,28},{5,29},{6,30},{7,31},{8,0},{9,1... | collective-permute-start | bytes 122888 | tf_op jit(solution)/shard_map/ppermute | solution.py:382
  129.1 1.8 %collective-permute-done.8 = f32[80,128]{1,0:T(8,128)S(1)} collective-permute-done((f32[80,128]{1,0:T(8,128)S(1)}, f32[80,128]{1,0:T(8,128)S(1)}, u32[]{:S(2)}, u32[]{:S(2)}) %collective-permute-start.8) | collective-permute-done | bytes 40992 | tf_op jit(solution)/shard_map/ppermute | solution.py:382
  131.4 2.9 %collective-permute-start.12 = (f32[80,128]{1,0:T(8,128)S(1)}, f32[80,128]{1,0:T(8,128)S(1)}, u32[]{:S(2)}, u32[]{:S(2)}) collective-permute-start(f32[80,128]{1,0:T(8,128)S(1)} %add_add_fusion.1), channel_id=1, source_target_pairs={{0,6},{1,7},{2,0},{3,1},{4,2},{5,3},{6,4},{7,5},{8,14},{9,15},{10,... | collective-permute-start | bytes 122888 | tf_op jit(solution)/shard_map/ppermute | solution.py:382
  134.3 0.9 collective-permute-start.13
  135.2 1.2 collective-permute-done.11
  136.3 3.4 %collective-permute-done.13 = f32[80,128]{1,0:T(8,128)S(1)} collective-permute-done((f32[80,128]{1,0:T(8,128)S(1)}, f32[80,128]{1,0:T(8,128)S(1)}, u32[]{:S(2)}, u32[]{:S(2)}) %collective-permute-start.13) | collective-permute-done | bytes 40992 | tf_op jit(solution)/shard_map/ppermute | solution.py:382
  (69 shorter events, 9.7 us)
Async XLA Ops:
  7.2 91.3 %all-gather.2.cloned.1.call-start = ((), (), s32[]{:S(2)}) async-start(), calls=%async_computation.2 | async-start | bytes 5013504 | tf_op jit(solution)/shard_map/all_gather | solution.py:416
  9.3 3.4 %copy-start.8 = (s32[9,3]{0,1:T(4,128)S(1)}, s32[9,3]{0,1:T(4,128)}, u32[]{:S(2)}) copy-start(s32[9,3]{0,1:T(4,128)} %param.12) | copy-start | bytes 328
  9.4 1.7 %collective-permute-start.1 = (bf16[12,2,16,384]{3,2,1,0:T(8,128)(2,1)S(1)}, bf16[12,2,16,384]{3,2,1,0:T(8,128)(2,1)S(1)}, u32[]{:S(2)}, u32[]{:S(2)}) collective-permute-start(bf16[12,2,16,384]{3,2,1,0:T(8,128)(2,1)S(1)} %copy.24), channel_id=1, source_target_pairs={{0,1},{1,0},{2,3},{3,2},{4,5},{5,4},{6,7},{7,6},{8,9},{9,8},{10,11... | collective-permute-start | bytes 884744 | tf_op jit(solution)/shard_map/ppermute | solution.py:411
  11.2 19.8 %copy-start = (bf16[24,2,16,384]{3,2,1,0:T(8,128)(2,1)}, bf16[24,2,16,384]{3,2,1,0:T(8,128)(2,1)S(1)}, u32[]{:S(2)}) copy-start(bf16[24,2,16,384]{3,2,1,0:T(8,128)(2,1)S(1)} %maximum_select_fusion.tau_ref) | copy-start | bytes 1769476
  12.5 4.7 %collective-permute-start = (bf16[1536,2,384]{2,0,1:T(8,128)(2,1)S(1)}, bf16[1536,2,384]{2,0,1:T(8,128)(2,1)}, u32[]{:S(2)}, u32[]{:S(2)}) collective-permute-start(bf16[1536,2,384]{2,0,1:T(8,128)(2,1)S(1)} %copy.29), channel_id=1, source_target_pairs={{0,1},{1,0},{2,3},{3,2},{4,5},{5,4},{6,7},{7,6},{8,9},{9,8},{10,11... | collective-permute-start | bytes 7077896 | tf_op jit(solution)/shard_map/ppermute | solution.py:408
  30.9 27.2 %all-to-all-start = ((bf16[16,24,1280]{2,1,0:T(8,128)(2,1)}), bf16[16,24,1280]{2,1,0:T(8,128)(2,1)S(1)}, u32[]{:S(2)}, u32[]{:S(2)}) async-start(bf16[16,24,1280]{2,1,0:T(8,128)(2,1)} %phase_0.1), calls=%async_computation | async-start | bytes 1966080 | tf_op jit(solution)/shard_map/all_to_all | solution.py:387
  58.1 7.4 %copy-start.7 = (f32[2,64,8]{1,2,0:T(8,128)S(1)}, f32[2,64,8]{1,2,0:T(8,128)}, u32[]{:S(2)}) copy-start(f32[2,64,8]{1,2,0:T(8,128)} %param.15) | copy-start | bytes 12292
  58.1 8.1 %copy-start.9 = (s32[64]{0:T(128)S(1)}, s32[64]{0:T(128)}, u32[]{:S(2)}) copy-start(s32[64]{0:T(128)} %param.13) | copy-start | bytes 772
  58.1 8.8 %copy-start.10 = (s32[64]{0:T(128)S(1)}, s32[64]{0:T(128)}, u32[]{:S(2)}) copy-start(s32[64]{0:T(128)} %param.14) | copy-start | bytes 772
  58.1 38.0 %all-to-all-start.1 = ((bf16[16,24,2432]{2,1,0:T(8,128)(2,1)}), bf16[16,24,2432]{2,1,0:T(8,128)(2,1)S(1)}, u32[]{:S(2)}, u32[]{:S(2)}) async-start(bf16[16,24,2432]{2,1,0:T(8,128)(2,1)} %phase_1.1), calls=%async_computation.1 | async-start | bytes 3735552 | tf_op jit(solution)/shard_map/all_to_all | solution.py:387
  68.2 9.7 %copy-start.4 = (bf16[24,1152]{1,0:T(8,128)(2,1)}, bf16[24,1152]{1,0:T(8,128)(2,1)S(1)}, u32[]{:S(2)}) copy-start(bf16[24,1152]{1,0:T(8,128)(2,1)S(1)} %fusion.1.own1) | copy-start | bytes 165892
  68.2 9.7 %collective-permute-start.2 = (bf16[24,1152]{1,0:T(8,128)(2,1)S(1)}, bf16[24,1152]{1,0:T(8,128)(2,1)S(1)}, u32[]{:S(2)}, u32[]{:S(2)}) collective-permute-start(bf16[24,1152]{1,0:T(8,128)(2,1)S(1)} %fusion.1.own1), channel_id=1, source_target_pairs={{0,1},{1,0},{2,3},{3,2},{4,5},{5,4},{6,7},{7,6},{8,9},{9,8},{10,11... | collective-permute-start | bytes 165896 | tf_op jit(solution)/shard_map/ppermute | solution.py:428
  77.8 20.7 %copy-start.6 = (bf16[24,1152]{1,0:T(8,128)(2,1)}, bf16[24,1152]{1,0:T(8,128)(2,1)S(1)}, u32[]{:S(2)}) copy-start(bf16[24,1152]{1,0:T(8,128)(2,1)S(1)} %collective-permute-done.2.oth1) | copy-start | bytes 165892
  96.9 1.6 %collective-permute-start.3 = (bf16[24,2304]{1,0:T(8,128)(2,1)S(1)}, bf16[24,2304]{1,0:T(8,128)(2,1)S(1)}, u32[]{:S(2)}, u32[]{:S(2)}) collective-permute-start(bf16[24,2304]{1,0:T(8,128)(2,1)S(1)} %fusion.own2), channel_id=1, source_target_pairs={{0,1},{1,0},{2,3},{3,2},{4,5},{5,4},{6,7},{7,6},{8,9},{9,8},{10,11... | collective-permute-start | bytes 331784 | tf_op jit(solution)/shard_map/ppermute | solution.py:431
  113.0 1.5 %collective-permute-start.4 = (f32[72,128]{1,0:T(8,128)}, f32[72,128]{1,0:T(8,128)S(1)}, u32[]{:S(2)}, u32[]{:S(2)}) collective-permute-start(f32[72,128]{1,0:T(8,128)} %sink.1), channel_id=1, source_target_pairs={{0,1},{1,0},{2,3},{3,2},{4,5},{5,4},{6,7},{7,6},{8,9},{9,8},{10,11... | collective-permute-start | bytes 110600 | tf_op jit(solution)/shard_map/ppermute | solution.py:433
  115.3 6.9 %collective-permute-start.5 = (f32[8,128]{1,0:T(8,128)S(1)}, f32[8,128]{1,0:T(8,128)S(1)}, u32[]{:S(2)}, u32[]{:S(2)}) collective-permute-start(f32[8,128]{1,0:T(8,128)S(1)} %slice.89), channel_id=1, source_target_pairs={{0,32},{1,33},{2,34},{3,35},{4,36},{5,37},{6,38},{7,39},{8,40},{9,... | collective-permute-start | bytes 12296 | tf_op jit(solution)/shard_map/ppermute | solution.py:437
  118.7 3.4 %collective-permute-start.6 = (f32[8,128]{1,0:T(8,128)S(1)}, f32[8,128]{1,0:T(8,128)S(1)}, u32[]{:S(2)}, u32[]{:S(2)}) collective-permute-start(f32[8,128]{1,0:T(8,128)S(1)} %slice.89), channel_id=1, source_target_pairs={{0,96},{1,97},{2,98},{3,99},{4,100},{5,101},{6,102},{7,103},{8,104... | collective-permute-start | bytes 12296 | tf_op jit(solution)/shard_map/ppermute | solution.py:437
  120.8 2.6 %collective-permute-start.7 = (f32[8,128]{1,0:T(8,128)S(1)}, f32[8,128]{1,0:T(8,128)S(1)}, u32[]{:S(2)}, u32[]{:S(2)}) collective-permute-start(f32[8,128]{1,0:T(8,128)S(1)} %slice.89), channel_id=1, source_target_pairs={{0,64},{1,65},{2,66},{3,67},{4,68},{5,69},{6,70},{7,71},{8,72},{9,... | collective-permute-start | bytes 12296 | tf_op jit(solution)/shard_map/ppermute | solution.py:437
  123.5 5.7 %collective-permute-start.10 = (f32[80,128]{1,0:T(8,128)S(1)}, f32[80,128]{1,0:T(8,128)S(1)}, u32[]{:S(2)}, u32[]{:S(2)}) collective-permute-start(f32[80,128]{1,0:T(8,128)S(1)} %pad_maximum_fusion), channel_id=1, source_target_pairs={{0,16},{1,17},{2,18},{3,19},{4,20},{5,21},{6,22},{7,23},{8,24},{9,... | collective-permute-start | bytes 122888 | tf_op jit(solution)/shard_map/ppermute | solution.py:382
  125.7 5.2 %collective-permute-start.8 = (f32[80,128]{1,0:T(8,128)S(1)}, f32[80,128]{1,0:T(8,128)S(1)}, u32[]{:S(2)}, u32[]{:S(2)}) collective-permute-start(f32[80,128]{1,0:T(8,128)S(1)} %pad_maximum_fusion), channel_id=1, source_target_pairs={{0,8},{1,9},{2,10},{3,11},{4,12},{5,13},{6,14},{7,15},{8,16},{9,17... | collective-permute-start | bytes 122888 | tf_op jit(solution)/shard_map/ppermute | solution.py:382
  125.9 5.0 %collective-permute-start.9 = (f32[80,128]{1,0:T(8,128)S(1)}, f32[80,128]{1,0:T(8,128)S(1)}, u32[]{:S(2)}, u32[]{:S(2)}) collective-permute-start(f32[80,128]{1,0:T(8,128)S(1)} %pad_maximum_fusion), channel_id=1, source_target_pairs={{0,24},{1,25},{2,26},{3,27},{4,28},{5,29},{6,30},{7,31},{8,0},{9,1... | collective-permute-start | bytes 122888 | tf_op jit(solution)/shard_map/ppermute | solution.py:382
  130.9 5.4 %collective-permute-start.11 = (f32[80,128]{1,0:T(8,128)S(1)}, f32[80,128]{1,0:T(8,128)S(1)}, u32[]{:S(2)}, u32[]{:S(2)}) collective-permute-start(f32[80,128]{1,0:T(8,128)S(1)} %add_add_fusion.1), channel_id=1, source_target_pairs={{0,2},{1,3},{2,4},{3,5},{4,6},{5,7},{6,0},{7,1},{8,10},{9,11},{10,... | collective-permute-start | bytes 122888 | tf_op jit(solution)/shard_map/ppermute | solution.py:382
  131.4 5.0 %collective-permute-start.12 = (f32[80,128]{1,0:T(8,128)S(1)}, f32[80,128]{1,0:T(8,128)S(1)}, u32[]{:S(2)}, u32[]{:S(2)}) collective-permute-start(f32[80,128]{1,0:T(8,128)S(1)} %add_add_fusion.1), channel_id=1, source_target_pairs={{0,6},{1,7},{2,0},{3,1},{4,2},{5,3},{6,4},{7,5},{8,14},{9,15},{10,... | collective-permute-start | bytes 122888 | tf_op jit(solution)/shard_map/ppermute | solution.py:382
  134.3 5.5 %collective-permute-start.13 = (f32[80,128]{1,0:T(8,128)S(1)}, f32[80,128]{1,0:T(8,128)S(1)}, u32[]{:S(2)}, u32[]{:S(2)}) collective-permute-start(f32[80,128]{1,0:T(8,128)S(1)} %add_add_fusion.1), channel_id=1, source_target_pairs={{0,4},{1,5},{2,6},{3,7},{4,0},{5,1},{6,2},{7,3},{8,12},{9,13},{10,... | collective-permute-start | bytes 122888 | tf_op jit(solution)/shard_map/ppermute | solution.py:382
  (4 other events, 7.6 us)
Sparse Core Ops, SparseCore 0:
  12.6 73.6 all-gather.1
